TPU v7x, 32 devices: a whole 2x2x4 slice. The times are simulated.
32 devices in a mesh: dp: 8 (over z, x), tensor: 4 (over y, core).
Axes of the slice: x: 2, y: 2, z: 4, core: 2. Of those that a mesh axis runs over, the one named last changes fastest.
Arguments:
- hidden_in: bfloat16 [32768, 768], P(('dp', 'tensor')), may hold values from -6 to 6
- cotangent: bfloat16 [32768, 768], P(('dp', 'tensor')), may hold values from -6 to 6
- lengths: int32 [32], P('dp'), may hold values from 31 to 1024, as said below
- latent: int32 [32, 1024], P('dp'), may hold values from 0 to 1, as said below
- ln1_gain: float32 [768], replicated, may hold values from 0.5 to 1.5
- ln1_bias: float32 [768], replicated, may hold values from -1.75 to 1.75
- w_qkv: float32 [3, 768, 768], P(None, 'dp', 'tensor'), may hold values from -0.3125 to 0.3125
- b_qv: float32 [2, 768], replicated, may hold values from -1.75 to 1.75
- w_out: float32 [768, 768], P('tensor', 'dp'), may hold values from -1.25 to 1.25
- b_out: float32 [768], replicated, may hold values from -1.75 to 1.75
- ln2_gain: float32 [768], replicated, may hold values from 0.5 to 1.5
- ln2_bias: float32 [768], replicated, may hold values from -1.75 to 1.75
- w_up: float32 [768, 3072], P('dp', 'tensor'), may hold values from -0.21875 to 0.21875
- b_up: float32 [3072], replicated, may hold values from -1.75 to 1.75
- w_down: float32 [3072, 768], P('tensor', 'dp'), may hold values from -0.109375 to 0.109375
- b_down: float32 [768], replicated, may hold values from -1.75 to 1.75
Outputs:
- hidden_out: bfloat16 [32768, 768], P(('dp', 'tensor'))
- grad_in: float32 [32768, 768], P(('dp', 'tensor'))
- grad_ln1_gain: float32 [768], replicated
- grad_ln1_bias: float32 [768], replicated
- grad_w_qkv: float32 [3, 768, 768], P(None, 'dp', 'tensor')
- grad_b_qv: float32 [2, 768], replicated
- grad_w_out: float32 [768, 768], P('tensor', 'dp')
- grad_b_out: float32 [768], replicated
- grad_ln2_gain: float32 [768], replicated
- grad_ln2_bias: float32 [768], replicated
- grad_w_up: float32 [768, 3072], P('dp', 'tensor')
- grad_b_up: float32 [3072], replicated
- grad_w_down: float32 [3072, 768], P('tensor', 'dp')
- grad_b_down: float32 [768], replicated
Inputs may be any that keep to these rules, and one draw needn't show every extreme that they name: `lengths`: A sequence's true length: a question of about 1024*30/1024 to 1024*400/1024 tokens, 0 to 6 latent thoughts and an answer, at most 1024; some sequence has exactly 1024, and some sequence has the shortest length, a shortest question and a one-token answer. `latent`: latent thoughts directly follow a sequence's question and lie within its true length.
All inputs are finite; a program needn't handle non-finite values.
Results may differ from a plain program's by a relative error of at most 0.015.
The roundings to bfloat16 on the way count: a program that leaves them out, or rounds other values in their place, can miss the bound.
Values may be sent and summed in bfloat16 or wider, within the bound.
No kernel may reach another device: no remote copies, remote signals or barrier semaphores. Data moves between devices by JAX's collectives and lax.ppermute only.
A program may use at most 320 MiB of HBM per device.

v0:
```python
import functools

import jax
import jax.numpy as jnp
from jax import lax
from jax.experimental import pallas as pl
from jax.experimental.pallas import tpu as pltpu
from jax.sharding import PartitionSpec as P

HEAD_DIM = 64
LEN = 1024
PAIR = 2 * HEAD_DIM
TILE = 256
NEG_BIG = -1e30
EPSILON = 1e-05
VMEM_BYTES = 66_900_000
BF = jnp.bfloat16
F32 = jnp.float32
BOTH = ("dp", "tensor")
ANY_SPEC = pl.BlockSpec(memory_space=pl.ANY)


def dot_nn(a, b):
    return lax.dot_general(a, b, (((1,), (0,)), ((), ())), preferred_element_type=F32)


def dot_nt(a, b):
    return lax.dot_general(a, b, (((1,), (1,)), ((), ())), preferred_element_type=F32)


def dot_tn(a, b):
    return lax.dot_general(a, b, (((0,), (0,)), ((), ())), preferred_element_type=F32)


def norm_parts(rows_in):
    center = rows_in - jnp.mean(rows_in, axis=-1, keepdims=True)
    spread = jnp.mean(center * center, axis=-1, keepdims=True)
    scale = lax.rsqrt(spread + EPSILON)
    return center * scale, scale


def norm_back(gy, normed, scale):
    mean_gy = jnp.mean(gy, axis=-1, keepdims=True)
    mean_gyn = jnp.mean(gy * normed, axis=-1, keepdims=True)
    return (gy - mean_gy - normed * mean_gyn) * scale


def col_sum(values):
    return jnp.sum(values, axis=0, keepdims=True)


def once(shape, index):
    return pl.BlockSpec(shape, index, pipeline_mode=pl.Buffered(1))


def params(side_effects=False):
    return pltpu.CompilerParams(
        dimension_semantics=("arbitrary",),
        vmem_limit_bytes=VMEM_BYTES,
        has_side_effects=side_effects,
    )


def cost(flops, moved, exps=0):
    return pl.CostEstimate(flops=int(flops), bytes_accessed=int(moved), transcendentals=int(exps))


def place_of(index):
    return (index >> 3) & 3, (index >> 2) & 1, (index >> 1) & 1, index & 1


def index_of(z, x, y, core):
    return (z << 3) | (x << 2) | (y << 1) | core


def exchange(array, flip):
    pairs = [(i, index_of(*flip(*place_of(i)))) for i in range(32)]
    return lax.ppermute(array, BOTH, pairs)


def flip_first(z, x, y, core):
    return (z, x, y ^ 1, core) if core else (z, x ^ 1, y, core)


def flip_second(z, x, y, core):
    return (z, x ^ 1, y, core) if core else (z, x, y ^ 1, core)


def flip_core(z, x, y, core):
    return z, x, y, core ^ 1


def flip_near(z, x, y, core):
    return z ^ 1, x, y, core


def flip_far(z, x, y, core):
    return z ^ 2, x, y, core


def sums_kernel(plan, *refs):
    count_in = sum(len(offsets) for offsets, _ in plan)
    outs = refs[count_in : count_in + len(plan)]
    scratch = refs[count_in + len(plan) :]
    position = 0
    for i, (offsets, count) in enumerate(plan):
        terms, _, sems, _ = scratch[4 * i : 4 * i + 4]
        for slot in range(count):
            for k, offset in enumerate(offsets):
                pltpu.make_async_copy(
                    refs[position + k].at[offset + slot], terms.at[slot, k], sems.at[slot]
                ).start()
        position += len(offsets)
    for i, (offsets, count) in enumerate(plan):
        terms, result, sems, out_sem = scratch[4 * i : 4 * i + 4]

        def body(slot, _, i=i, size=len(offsets)):
            terms, result, sems, out_sem = scratch[4 * i : 4 * i + 4]
            wait_all(terms.at[slot], sems.at[slot])
            total = terms[slot, 0].astype(F32)
            for k in range(1, size):
                total = total + terms[slot, k].astype(F32)
            result[slot] = total.astype(BF)
            pltpu.make_async_copy(result.at[slot], outs[i].at[slot], out_sem).start()
            return 0

        lax.fori_loop(0, count, body, 0)
    for i in range(len(plan)):
        wait_all(scratch[4 * i + 1], scratch[4 * i + 3])


def sums(*requests):
    plan, arrays, shapes, scratch = [], [], [], []
    for terms, count in requests:
        block = terms[0][0].shape[1:]
        plan.append((tuple(offset for _, offset in terms), count))
        arrays += [array for array, _ in terms]
        shapes.append(jax.ShapeDtypeStruct((count, *block), BF))
        scratch += [
            pltpu.VMEM((count, len(terms), *block), BF),
            pltpu.VMEM((count, *block), BF),
            pltpu.SemaphoreType.DMA((count,)),
            pltpu.SemaphoreType.DMA(()),
        ]
    return pl.pallas_call(
        functools.partial(sums_kernel, plan),
        in_specs=[ANY_SPEC] * len(arrays),
        out_specs=[ANY_SPEC] * len(shapes),
        out_shape=shapes,
        scratch_shapes=scratch,
        compiler_params=pltpu.CompilerParams(vmem_limit_bytes=VMEM_BYTES),
        cost_estimate=cost(1e6, 8e6),
        name="sums",
    )(*arrays)


def plain_sums(*requests):
    results = []
    for terms, count in requests:
        total = None
        for array, offset in terms:
            part = array[offset : offset + count].astype(F32)
            total = part if total is None else total + part
        results.append(total.astype(BF))
    return results


def split_columns(up, rest):
    width = up.shape[1] - PAIR
    side = 3 * PAIR
    out = jnp.concatenate([up[:, width:], rest[:, side + 3 * HEAD_DIM :]], axis=1)
    three = []
    for i in range(3):
        begin = side + i * HEAD_DIM
        parts = [rest[:, i * PAIR : (i + 1) * PAIR], rest[:, begin : begin + HEAD_DIM]]
        three.append(jnp.concatenate(parts, axis=1))
    return out, jnp.stack(three)


def last_kernel(counts, *refs):
    sources, rest_of = refs[: sum(counts)], refs[sum(counts) :]
    up_ref, out_ref, down_ref, qkv_ref = rest_of[:4]
    scratch, sems = rest_of[4:7], rest_of[7]
    position = 0
    for i, count in enumerate(counts):
        for k in range(count):
            pltpu.make_async_copy(
                sources[position + k].at[0], scratch[i].at[k], sems.at[i]
            ).start()
        position += count
    totals = []
    for i, count in enumerate(counts):
        wait_all(scratch[i], sems.at[i])
        total = scratch[i][0].astype(F32)
        for k in range(1, count):
            total = total + scratch[i][k].astype(F32)
        totals.append(total)
    up, down, rest = totals
    up_ref[...] = up[:, : up_ref.shape[1]]
    down_ref[...] = down
    out, qkv_ref[...] = split_columns(up, rest)
    out_ref[...] = jnp.transpose(out)


def last_sums(*chains):
    counts = [len(terms) for terms in chains]
    block = chains[0][0].shape[1]
    width, third = chains[1][0].shape[2], 3 * HEAD_DIM
    whole = pl.BlockSpec(memory_space=pltpu.VMEM)
    return pl.pallas_call(
        functools.partial(last_kernel, counts),
        in_specs=[ANY_SPEC] * sum(counts),
        out_specs=[whole] * 4,
        out_shape=[
            jax.ShapeDtypeStruct((block, width), F32),
            jax.ShapeDtypeStruct((third, block), F32),
            jax.ShapeDtypeStruct((block, width), F32),
            jax.ShapeDtypeStruct((3, block, third), F32),
        ],
        scratch_shapes=[
            pltpu.VMEM((len(terms), block, terms[0].shape[2]), BF) for terms in chains
        ]
        + [pltpu.SemaphoreType.DMA((3,))],
        compiler_params=pltpu.CompilerParams(vmem_limit_bytes=VMEM_BYTES),
        cost_estimate=cost(1e6, 4e6),
        name="last_sums",
    )(*(term for terms in chains for term in terms))


class Scatter:
    def __init__(self, kept, sent):
        self.terms, self.sent = [kept], sent
        self.flips = [flip_core, flip_second, flip_first, flip_far, flip_near]

    def step(self):
        return exchange(self.sent, self.flips.pop(0))

    def want(self, came):
        self.terms = [*self.terms, came]
        count = came.shape[0] // 2
        return [(array, count) for array in self.terms], count


def after(value, *others):
    return lax.optimization_barrier((value, *others))


def ring_place(z):
    z = z & 3
    return z ^ (z >> 1)


def flip_ring(z, x, y, core):
    return ring_place(ring_place(z) + 1), x, y, core


def start_blocks(place_ref, sources, cols, raw, to, sems, order="xor"):
    if len(sources) == 1:
        nd, blocks, block, _ = sources[0].shape
        for d in range(nd):
            for t in range(blocks):
                pltpu.make_async_copy(
                    sources[0].at[d, t, :, cols],
                    raw.at[t, d * block : (d + 1) * block, to],
                    sems.at[t],
                ).start()
        return
    z, x, y, core = (place_ref[i] for i in range(4))
    block = sources[0].shape[1]
    for i, source in enumerate(sources):
        for slot in range(4):
            to_core = core ^ (i >> 2)
            pair, step = (slot, i & 3) if order == "last" else (i & 3, slot)
            second, first = pair >> 1, pair & 1
            to_x = x ^ (first + to_core * (second - first))
            to_y = y ^ (second + to_core * (first - second))
            to_z = z ^ step if order == "xor" else ring_place(ring_place(z) - step)
            to_t = to_y * 2 + to_core
            low = pl.multiple_of((to_z * 2 + to_x) * block, block)
            pltpu.make_async_copy(
                source.at[slot, :, cols], raw.at[to_t, pl.ds(low, block), to], sems.at[to_t]
            ).start()


def wait_all(ref, sem):
    pltpu.make_async_copy(ref, ref, sem).wait()


def send_block(place_ref, staged, outs, sem, d, t, ring):
    z, x, y, core = (place_ref[i] for i in range(4))
    far, near_core = d >> 1, t & 1
    x_off, y_off = x ^ (d & 1), y ^ (t >> 1)
    first, second = (y_off, x_off) if near_core else (x_off, y_off)
    along = (ring_place(far) - ring_place(z)) & 3 if ring else z ^ far
    slot = second * 8 + first * 4 + along
    for side in range(2):

        @pl.when((core ^ near_core) == side)
        def _(side=side):
            pltpu.make_async_copy(staged, outs[side].at[slot], sem).start()


def send_rows(place_ref, stage, outs, sem, t, cols, part=None, ring=False):
    if len(outs) == 1:
        half = stage.shape[0] // 2
        rows = slice(None) if part is None else slice(part * half, (part + 1) * half)
        pltpu.make_async_copy(stage.at[rows, :], outs[0].at[t, rows, cols], sem).start()
        return
    block = outs[0].shape[1]
    for d in range(8) if part is None else range(4 * part, 4 * part + 4):
        staged = stage.at[d * block : (d + 1) * block, :]
        send_block(place_ref, staged, [out.at[:, :, cols] for out in outs], sem, d, t, ring)


def qkv_kernel(count, place_ref, x_ref, gain_ref, bias_ref, bqv_ref, *refs):
    sources = refs[:count]
    q_ref, k_ref, v_ref, n_ref, w_out, raw, sems, w_ref, w_sem = refs[count:]
    blocks = raw.shape[0]
    normed, _ = norm_parts(x_ref[...].astype(F32))
    low = (normed * gain_ref[...] + bias_ref[...]).astype(BF)
    n_ref[...] = low

    @pl.when(pl.program_id(0) == 0)
    def _():
        cols = slice(0, raw.shape[2])
        start_blocks(place_ref, sources, cols, raw, cols, sems)
        for t in range(blocks):
            wait_all(raw.at[t], sems.at[t])

        def piece(t, c):
            return raw[t, :, c * PAIR : (c + 1) * PAIR]

        for t in range(blocks):
            for c in range(4):
                w_ref[c, :, t * PAIR : (t + 1) * PAIR] = piece(t, c)
        for u in range(blocks // 2):
            col = (blocks + u) * PAIR
            for half in range(2):
                left = piece(2 * u, 4 + half)
                right = piece(2 * u + 1, 4 + half)
                w_ref[2 * half, :, col : col + PAIR] = jnp.concatenate(
                    [left[:, :HEAD_DIM], right[:, :HEAD_DIM]], axis=1
                )
                w_ref[2 * half + 1, :, col : col + PAIR] = jnp.concatenate(
                    [left[:, HEAD_DIM:], right[:, HEAD_DIM:]], axis=1
                )
        pltpu.make_async_copy(w_ref, w_out, w_sem).start()

    q_low = (dot_nn(low, w_ref[0]) + bqv_ref[0:1, :]).astype(BF)
    q_ref[...] = q_low * BF(HEAD_DIM ** (-0.5))
    k_ref[...] = dot_nn(low, w_ref[1]).astype(BF)
    v_ref[...] = (dot_nn(low, w_ref[2]) + bqv_ref[1:2, :]).astype(BF)

    @pl.when(pl.program_id(0) == pl.num_programs(0) - 1)
    def _():
        wait_all(w_ref, w_sem)


def project(place, x, gain, bias, bqv, sources, blocks):
    rows, width = x.shape
    row_spec = pl.BlockSpec((TILE, width), lambda i, *_: (i, 0))
    return pl.pallas_call(
        functools.partial(qkv_kernel, len(sources)),
        grid_spec=pltpu.PrefetchScalarGridSpec(
            num_scalar_prefetch=1,
            grid=(rows // TILE,),
            in_specs=[
                row_spec,
                once((1, width), lambda i, *_: (0, 0)),
                once((1, width), lambda i, *_: (0, 0)),
                once((2, width), lambda i, *_: (0, 0)),
            ]
            + [ANY_SPEC] * len(sources),
            out_specs=[row_spec] * 4 + [ANY_SPEC],
            scratch_shapes=[
                pltpu.VMEM((blocks, width, sources[0].shape[-1]), BF),
                pltpu.SemaphoreType.DMA((blocks,)),
                pltpu.VMEM((4, width, width), BF),
                pltpu.SemaphoreType.DMA(()),
            ],
        ),
        out_shape=[jax.ShapeDtypeStruct((rows, width), BF)] * 4
        + [jax.ShapeDtypeStruct((4, width, width), BF)],
        compiler_params=params(),
        cost_estimate=cost(6 * rows * width * width, 16 * rows * width),
        name="project",
    )(place, x, gain, bias, bqv, *sources)


def half_masks():
    lane = lax.broadcasted_iota(jnp.int32, (1, PAIR), 1)
    first = (lane < HEAD_DIM).astype(F32)
    return first.astype(BF), (1.0 - first).astype(BF)


def attend_kernel(len_ref, q_ref, k_ref, v_ref, o_ref, lse_ref):
    rows = q_ref.shape[0]
    length = len_ref[0]
    masks = half_masks()
    lane = lax.broadcasted_iota(jnp.int32, (TILE, PAIR), 1)
    k_pos = lax.broadcasted_iota(jnp.int32, (1, rows), 1)
    bias = jnp.where(k_pos < length, 0.0, NEG_BIG)
    tri = lax.broadcasted_iota(jnp.int32, (TILE, TILE), 0) >= lax.broadcasted_iota(
        jnp.int32, (TILE, TILE), 1
    )
    for n in range(0, rows, TILE):
        q_block = q_ref[n : n + TILE, :]
        scores = []
        for mask in masks:
            q_one = q_block * mask
            s_diag = dot_nt(q_one, k_ref[n : n + TILE, :]) + bias[:, n : n + TILE]
            s_diag = jnp.where(tri, s_diag, NEG_BIG)
            s_rest = dot_nt(q_one, k_ref[:n, :]) + bias[:, :n] if n else None
            scores.append((s_diag, s_rest))
        outs = []
        peaks = []
        totals = []
        for s_diag, s_rest in scores:
            peak = jnp.max(s_diag, axis=1, keepdims=True)
            if n:
                peak = jnp.maximum(peak, jnp.max(s_rest, axis=1, keepdims=True))
            e_diag = jnp.exp(s_diag - peak)
            total = jnp.sum(e_diag, axis=1, keepdims=True)
            acc = dot_nn(e_diag.astype(BF), v_ref[n : n + TILE, :])
            if n:
                e_rest = jnp.exp(s_rest - peak)
                total = total + jnp.sum(e_rest, axis=1, keepdims=True)
                acc = acc + dot_nn(e_rest.astype(BF), v_ref[:n, :])
            outs.append(acc)
            peaks.append(peak)
            totals.append(total)
        first = lane < HEAD_DIM
        both = jnp.where(first, outs[0], outs[1])
        o_ref[n : n + TILE, :] = (both / jnp.where(first, totals[0], totals[1])).astype(BF)
        packed = jnp.where(lane < 8, peaks[0], totals[0])
        packed = jnp.where(lane % 8 == 1, jnp.where(lane < 8, peaks[1], totals[1]), packed)
        flipped = jnp.transpose(packed)
        lse_ref[0, :, n : n + TILE] = flipped[:8, :] + jnp.log(flipped[8:16, :])


def attend(lengths, q, k, v):
    rows, width = q.shape
    pairs = width // PAIR
    pair_spec = pl.BlockSpec((rows, PAIR), lambda i, *_: (0, i))
    return pl.pallas_call(
        attend_kernel,
        grid_spec=pltpu.PrefetchScalarGridSpec(
            num_scalar_prefetch=1,
            grid=(pairs,),
            in_specs=[pair_spec] * 3,
            out_specs=[pair_spec, pl.BlockSpec((1, 8, rows), lambda i, *_: (i, 0, 0))],
        ),
        out_shape=[
            jax.ShapeDtypeStruct((rows, width), BF),
            jax.ShapeDtypeStruct((pairs, 8, rows), F32),
        ],
        compiler_params=params(),
        cost_estimate=cost(16e9 * width / 768, 8 * rows * width),
        name="attend",
    )(lengths, q, k, v)


def attend_back_kernel(
    first, n_out, more, len_ref, place_ref, q_ref, k_ref, v_ref, o_ref, do_ref, lse_ref, n_ref,
    out_ref, *refs
):
    refs = refs[n_out:] if more else refs
    dq_ref, dk_ref, dv_ref = refs[:3]
    outs = refs[3 : 3 + n_out]
    dq_acc, side_s, n_s, stage, n_sem, sem = refs[3 + n_out :]
    rows = q_ref.shape[0]
    width = n_ref.shape[1]
    step = pl.program_id(0)
    length = len_ref[0]
    masks = half_masks()
    wide = stage.shape[2]
    narrow = wide != 3 * PAIR

    @pl.when(step == 0)
    def _():
        pltpu.make_async_copy(n_ref, n_s, n_sem).start()

    prod = jnp.transpose(do_ref[...].astype(F32) * o_ref[...].astype(F32))
    tri = lax.broadcasted_iota(jnp.int32, (TILE, TILE), 0) <= lax.broadcasted_iota(
        jnp.int32, (TILE, TILE), 1
    )
    k_pos = lax.broadcasted_iota(jnp.int32, (TILE, 1), 0)
    dq_acc[...] = jnp.zeros_like(dq_acc)
    heads = []
    for h, mask in enumerate(masks):
        heads.append(
            (
                mask,
                q_ref[...] * mask,
                do_ref[...] * mask,
                lse_ref[0, h : h + 1, :],
                jnp.sum(prod[h * HEAD_DIM : (h + 1) * HEAD_DIM, :], axis=0, keepdims=True),
            )
        )
    for n in range(0, rows, TILE):
        k_block = k_ref[n : n + TILE, :]
        v_block = v_ref[n : n + TILE, :]
        bias = jnp.where(k_pos + n < length, 0.0, NEG_BIG)
        dk = jnp.zeros((TILE, PAIR), F32)
        dv = jnp.zeros((TILE, PAIR), F32)
        work = []
        for mask, q_one, do_one, lse, delta in heads:
            for low, high in ((n, n + TILE), (n + TILE, rows)):
                if low == high:
                    continue
                s = dot_nt(k_block, q_one[low:high]) + bias
                dp = dot_nt(v_block, do_one[low:high])
                work.append((mask, q_one, do_one, lse, delta, low, high, s, dp))
        for mask, q_one, do_one, lse, delta, low, high, s, dp in work:
            if low == n:
                s = jnp.where(tri, s, NEG_BIG)
            p = jnp.exp(s - lse[:, low:high])
            ds = (p * (dp - delta[:, low:high])).astype(BF)
            dv = dv + dot_nn(p.astype(BF), do_one[low:high])
            dk = dk + dot_nn(ds, q_one[low:high])
            dq_acc[low:high, :] += dot_tn(ds, k_block * mask)
        dk_ref[n : n + TILE, :] = dk.astype(BF)
        dv_ref[n : n + TILE, :] = dv.astype(BF)
    dq_ref[...] = (dq_acc[...] * (HEAD_DIM ** (-0.5))).astype(BF)

    grads = [dq_ref[...], dk_ref[...], dv_ref[...]]
    if narrow:
        blank = jnp.zeros((rows, HEAD_DIM), BF)
        sides = [
            jnp.concatenate([g[:, c : c + HEAD_DIM] for g in grads] + [blank], axis=1)
            for c in (0, HEAD_DIM)
        ]
    else:
        sides = [jnp.concatenate(grads, axis=1)]
    pairs = side_s.shape[1] // (wide * len(sides))
    for at in range(pairs):

        @pl.when(step == at)
        def _(at=at):
            for i, side in enumerate(sides):
                spot = at * len(sides) + i
                side_s[:, spot * wide : (spot + 1) * wide] = side

    @pl.when(step == pairs - 1)
    def _():
        pltpu.make_async_copy(n_ref, n_s, n_sem).wait()
        low_col = 3 * PAIR if narrow else 0
        columns = slice(low_col, low_col + wide)
        for part in range(2):
            cols = slice(part * width // 2, (part + 1) * width // 2)
            grad = dot_tn(n_s[:, cols], side_s[...]).astype(BF)
            for spot in range(stage.shape[0]):
                t = spot if narrow else first + spot
                begin = spot * wide
                if narrow:
                    stage[spot, cols, :PAIR] = grad[:, begin : begin + PAIR]
                    extra = out_ref[cols, spot * HEAD_DIM : (spot + 1) * HEAD_DIM]
                    stage[spot, cols, PAIR:] = jnp.concatenate(
                        [grad[:, begin + PAIR : begin + PAIR + HEAD_DIM], extra], axis=1
                    )
                else:
                    stage[spot, cols, :] = grad[:, begin : begin + wide]
                send_rows(place_ref, stage.at[spot], outs, sem, t, columns, part)
        wait_all(stage, sem)


def attend_back(
    place, lengths, first, pairs, wide, q, k, v, out, d_out, lse, normed, last_out, blocks,
    so_far, fast,
):
    rows, width = q.shape
    at_pair = pl.BlockSpec((rows, PAIR), lambda i, *_: (0, first + i))
    own_pair = pl.BlockSpec((rows, PAIR), lambda i, *_: (0, i))
    grads = grad_shapes(fast, blocks, width, 5 * PAIR)
    so_far = so_far or []
    sides = 1 if wide == 3 * PAIR else 2
    return pl.pallas_call(
        functools.partial(attend_back_kernel, first, len(grads), bool(so_far)),
        grid_spec=pltpu.PrefetchScalarGridSpec(
            num_scalar_prefetch=2,
            grid=(pairs,),
            in_specs=[at_pair] * 5
            + [
                pl.BlockSpec((1, 8, rows), lambda i, *_: (first + i, 0, 0)),
                ANY_SPEC,
                once(last_out.shape, lambda i, *_: (0, 0)),
            ]
            + [ANY_SPEC] * len(so_far),
            out_specs=[own_pair] * 3 + [ANY_SPEC] * len(grads),
            scratch_shapes=[
                pltpu.VMEM((rows, PAIR), F32),
                pltpu.VMEM((rows, pairs * sides * wide), BF),
                pltpu.VMEM((rows, width), BF),
                pltpu.VMEM((pairs * sides, width, wide), BF),
                pltpu.SemaphoreType.DMA(()),
                pltpu.SemaphoreType.DMA(()),
            ],
        ),
        out_shape=[jax.ShapeDtypeStruct((rows, pairs * PAIR), BF)] * 3 + grads,
        input_output_aliases={10 + i: 3 + i for i in range(len(so_far))},
        compiler_params=params(),
        cost_estimate=cost(3e9 * pairs, 5e6 * pairs),
        name="attend_back",
    )(lengths, place, q, k, v, out, d_out, lse, normed, last_out, *so_far)


def vec_rows(vec_ref):
    return lambda i: vec_ref[i : i + 1, :]


def tile_rows(i):
    return pl.ds(pl.multiple_of(i * TILE, TILE), TILE)


def grad_shapes(fast, blocks, width, wide):
    if fast:
        return [jax.ShapeDtypeStruct((16, width // 8, wide), BF)] * 2
    return [jax.ShapeDtypeStruct((blocks, width, wide), BF)]


def feed_kernel(
    counts, place_ref, att_ref, x_ref, cot_ref, wo_ref, vec_ref, bup_ref, *refs
):
    one, two = counts
    refs, sources = refs[one + two :], (refs[:one], refs[one : one + two])
    resid_out, act_ref, gbup_ref, dres_out, datt_out, sums_ref, last_out_ref = refs[:7]
    refs = refs[7:]
    n_out = (len(refs) - 13) // 2
    up_outs, down_outs = refs[:n_out], refs[n_out : 2 * n_out]
    raw, sems, n_two, d_pre_s, d_norm, low, stage, stage_down, sem = refs[2 * n_out : -4]
    resid_ref, dres_ref, datt_ref, out_sems = refs[-4:]
    rows, width = x_ref.shape
    step = pl.program_id(0)
    tiles = rows // TILE
    blocks = stage.shape[0]
    vec = vec_rows(vec_ref)
    half_width = width // 2
    cut = sources[0][0].shape[-1] // 2

    @pl.when(step == 0)
    def _():
        begin = 0
        sizes, orders = (cut, width - cut), ("ring", "last")
        for source, size, order in zip(sources, sizes, orders, strict=True):
            for to in (begin, width + begin):
                start_blocks(
                    place_ref,
                    source,
                    slice(0 if to < width else size, size if to < width else 2 * size),
                    raw,
                    slice(to, to + size),
                    sems,
                    order,
                )
            begin += size

        def body(i, _):
            r = tile_rows(i)
            res = x_ref[r, :].astype(F32) + dot_nt(att_ref[r, :], wo_ref[0]) + vec(0)
            resid_ref[r, :] = res
            normed, _ = norm_parts(res)
            n_two[r, :] = (normed * vec(1) + vec(2)).astype(BF)
            d_norm[r, :] = jnp.zeros((TILE, width), F32)
            return 0

        lax.fori_loop(0, tiles, body, 0)
        pltpu.make_async_copy(resid_ref, resid_out, out_sems.at[0]).start()

    wait_all(raw.at[step], sems.at[step])
    w_up = raw[step, :, :width]
    w_down = raw[step, :, width:]
    c_one = 0.7978845608028654
    c_two = 0.044715

    def body(i, total):
        r = tile_rows(i)
        u = dot_nn(n_two[r, :], w_up) + bup_ref[0]
        d_act = dot_nn(cot_ref[r, :], w_down)
        square = u * u
        t = jnp.tanh(c_one * u * (1.0 + c_two * square))
        half = 0.5 * (1.0 + t)
        act_ref[r, :] = (u * half).astype(BF)
        slope = half + 0.5 * u * (1.0 - t * t) * (c_one * (1.0 + 3.0 * c_two * square))
        d_pre = (d_act * slope).astype(BF)
        d_pre_s[r, :] = d_pre
        d_norm[r, :] += dot_nt(d_pre, w_up)
        return total + col_sum(d_pre.astype(F32))

    gbup_ref[0] = lax.fori_loop(0, tiles, body, jnp.zeros((1, width), F32), unroll=True)
    def grads(i, _):
        cols = tile_rows(i)
        stage[step, cols, :width] = dot_tn(n_two[:, cols], d_pre_s[...]).astype(BF)
        stage_down[step, cols, :] = dot_tn(cot_ref[:, cols], act_ref[...]).astype(BF)
        return 0

    lax.fori_loop(0, width // TILE, grads, 0)
    first_cols = slice(0, width)
    for t in range(blocks):

        @pl.when(step == t)
        def _(t=t):
            send_rows(place_ref, stage.at[t, :, first_cols], up_outs, sem, t, first_cols)
            send_rows(place_ref, stage_down.at[t], down_outs, sem, t, first_cols)

    @pl.when(step == pl.num_programs(0) - 1)
    def _():
        def body(i, sums):
            r = tile_rows(i)
            normed, scale = norm_parts(resid_ref[r, :])
            d_n = d_norm[r, :]
            d_out = cot_ref[r, :].astype(F32)
            d_res = d_out + norm_back(d_n * vec(1), normed, scale)
            dres_ref[r, :] = d_res
            d_low = d_res.astype(BF)
            low[r, :] = d_low
            datt_ref[r, :] = dot_nn(d_low, wo_ref[0]).astype(BF)
            pltpu.make_async_copy(dres_ref.at[r, :], dres_out.at[r, :], out_sems.at[1]).start()
            pltpu.make_async_copy(datt_ref.at[r, :], datt_out.at[r, :], out_sems.at[2]).start()
            more = (col_sum(d_n * normed), col_sum(d_n), col_sum(d_res), col_sum(d_out))
            return tuple(a + b for a, b in zip(sums, more, strict=True))

        sums = lax.fori_loop(0, tiles, body, (jnp.zeros((1, width), F32),) * 4)
        sums_ref[...] = jnp.zeros_like(sums_ref)
        for i in range(4):
            sums_ref[i : i + 1, :] = sums[i]
        side = width
        for c in range(0, width, half_width):
            rows_c = slice(c, c + half_width)
            go = dot_tn(low[:, rows_c], att_ref[...]).astype(BF)
            last_out_ref[rows_c, :] = go[:, blocks * PAIR :]
            for t in range(blocks):
                stage[t, rows_c, side:] = go[:, t * PAIR : (t + 1) * PAIR]
        cols = slice(side, side + PAIR)
        for t in range(blocks):
            send_rows(place_ref, stage.at[t, :, cols], up_outs, sem, t, cols)
        wait_all(stage, sem)
        wait_all(stage_down, sem)
        for i, ref in enumerate((resid_ref, dres_ref, datt_ref)):
            wait_all(ref, out_sems.at[i])


def feed_forward(place, att, x, cot, w_all, vecs, b_up, sources_one, sources_two, fast):
    rows, width = x.shape
    blocks = b_up.shape[0]
    whole = once((rows, width), lambda t, *_: (0, 0))
    up_vec = pl.BlockSpec((1, 1, width), lambda t, *_: (t, 0, 0))
    grads = grad_shapes(fast, blocks, width, width + PAIR)
    grads += grad_shapes(fast, blocks, width, width)
    counts = (len(sources_one), len(sources_two))
    return pl.pallas_call(
        functools.partial(feed_kernel, counts),
        grid_spec=pltpu.PrefetchScalarGridSpec(
            num_scalar_prefetch=1,
            grid=(blocks,),
            in_specs=[
                whole,
                whole,
                whole,
                once((1, width, width), lambda t, *_: (3, 0, 0)),
                once((8, width), lambda t, *_: (0, 0)),
                up_vec,
            ]
            + [ANY_SPEC] * sum(counts),
            out_specs=[
                ANY_SPEC,
                pl.BlockSpec((rows, width), lambda t, *_: (0, t)),
                up_vec,
                ANY_SPEC,
                ANY_SPEC,
                once((8, width), lambda t, *_: (0, 0)),
                once((width, width - blocks * PAIR), lambda t, *_: (0, 0)),
            ]
            + [ANY_SPEC] * len(grads),
            scratch_shapes=[
                pltpu.VMEM((blocks, width, 2 * width), BF),
                pltpu.SemaphoreType.DMA((blocks,)),
                pltpu.VMEM((rows, width), BF),
                pltpu.VMEM((rows, width), BF),
                pltpu.VMEM((rows, width), F32),
                pltpu.VMEM((rows, width), BF),
                pltpu.VMEM((blocks, width, width + PAIR), BF),
                pltpu.VMEM((blocks, width, width), BF),
                pltpu.SemaphoreType.DMA(()),
                pltpu.VMEM((rows, width), F32),
                pltpu.VMEM((rows, width), F32),
                pltpu.VMEM((rows, width), BF),
                pltpu.SemaphoreType.DMA((3,)),
            ],
        ),
        out_shape=[
            jax.ShapeDtypeStruct((rows, width), F32),
            jax.ShapeDtypeStruct((rows, blocks * width), BF),
            jax.ShapeDtypeStruct((blocks, 1, width), F32),
            jax.ShapeDtypeStruct((rows, width), F32),
            jax.ShapeDtypeStruct((rows, width), BF),
            jax.ShapeDtypeStruct((8, width), F32),
            jax.ShapeDtypeStruct((width, width - blocks * PAIR), BF),
        ]
        + grads,
        compiler_params=params(),
        cost_estimate=cost(40e9, 40e6),
        name="feed_forward",
    )(place, att, x, cot, w_all, vecs, b_up, *sources_one, *sources_two)


def hidden_kernel(counts, place_ref, act_ref, resid_ref, vec_ref, *refs):
    one, two = counts
    refs, sources = refs[one + two :], (refs[:one], refs[one : one + two])
    out_ref, raw, sems = refs
    blocks, _, width = raw.shape
    cut = sources[0][0].shape[-1] // 2

    @pl.when(pl.program_id(0) == 0)
    def _():
        begin = 0
        sizes, orders = (cut, width - cut), ("ring", "last")
        for source, size, order in zip(sources, sizes, orders, strict=True):
            to = slice(begin, begin + size)
            start_blocks(place_ref, source, slice(size, 2 * size), raw, to, sems, order)
            begin += size
        for t in range(blocks):
            wait_all(raw.at[t], sems.at[t])

    acc = resid_ref[...] + vec_ref[3:4, :]
    for t in range(blocks):
        acc = acc + dot_nt(act_ref[:, t * width : (t + 1) * width], raw[t])
    out_ref[...] = acc.astype(BF)


def hidden_rows(place, act, resid, vecs, sources_one, sources_two):
    rows, width = resid.shape
    blocks = act.shape[1] // width
    row_spec = pl.BlockSpec((TILE, width), lambda i, *_: (i, 0))
    counts = (len(sources_one), len(sources_two))
    return pl.pallas_call(
        functools.partial(hidden_kernel, counts),
        grid_spec=pltpu.PrefetchScalarGridSpec(
            num_scalar_prefetch=1,
            grid=(rows // TILE,),
            in_specs=[
                pl.BlockSpec((TILE, blocks * width), lambda i, *_: (i, 0)),
                row_spec,
                once((8, width), lambda i, *_: (0, 0)),
            ]
            + [ANY_SPEC] * sum(counts),
            out_specs=row_spec,
            scratch_shapes=[
                pltpu.VMEM((blocks, width, width), BF),
                pltpu.SemaphoreType.DMA((blocks,)),
            ],
        ),
        out_shape=jax.ShapeDtypeStruct((rows, width), BF),
        compiler_params=params(),
        cost_estimate=cost(5e9, 12e6),
        name="hidden_rows",
    )(place, act, resid, vecs, *sources_one, *sources_two)


def input_kernel(*refs):
    parts = refs[:6]
    w_ref, x_ref, dres_ref, gain_ref, gin_ref, sums_ref = refs[6:]

    @pl.when(pl.program_id(0) == 0)
    def _():
        sums_ref[...] = jnp.zeros_like(sums_ref)

    dq, dk, dv = (jnp.concatenate([part[...] for part in parts[i::3]], axis=1) for i in range(3))
    d_norm = dot_nt(dq, w_ref[0]) + dot_nt(dk, w_ref[1]) + dot_nt(dv, w_ref[2])
    normed, scale = norm_parts(x_ref[...].astype(F32))
    gin_ref[...] = dres_ref[...] + norm_back(d_norm * gain_ref[...], normed, scale)
    more = (
        col_sum(d_norm * normed),
        col_sum(d_norm),
        col_sum(dq.astype(F32)),
        col_sum(dv.astype(F32)),
    )
    for i, value in enumerate(more):
        sums_ref[i : i + 1, :] += value


def input_grad(parts, w_all, x, d_resid, gain):
    rows, width = x.shape
    row_spec = pl.BlockSpec((TILE, width), lambda i: (i, 0))
    return pl.pallas_call(
        input_kernel,
        grid=(rows // TILE,),
        in_specs=[pl.BlockSpec((TILE, part.shape[1]), lambda i: (i, 0)) for part in parts]
        + [
            once((3, width, width), lambda i: (0, 0, 0)),
            row_spec,
            row_spec,
            once((1, width), lambda i: (0, 0)),
        ],
        out_specs=[row_spec, pl.BlockSpec((8, width), lambda i: (0, 0))],
        out_shape=[
            jax.ShapeDtypeStruct((rows, width), F32),
            jax.ShapeDtypeStruct((8, width), F32),
        ],
        compiler_params=params(),
        cost_estimate=cost(6 * rows * width * width, 16 * rows * width),
        name="input_grad",
    )(*parts, w_all, x, d_resid, gain)


def body(
    n_dp,
    n_tensor,
    hidden_in,
    cotangent,
    lengths,
    latent,
    ln1_gain,
    ln1_bias,
    w_qkv,
    b_qv,
    w_out,
    b_out,
    ln2_gain,
    ln2_bias,
    w_up,
    b_up,
    w_down,
    b_down,
):
    rows, width = hidden_in.shape
    t_index = lax.axis_index("tensor")
    block = w_up.shape[0]
    heads = w_qkv.shape[2] // HEAD_DIM

    out_t = w_out.T
    packed = jnp.concatenate(
        [w_qkv[0, :, :PAIR], w_qkv[1, :, :PAIR], w_qkv[2, :, :PAIR], out_t[:, :PAIR]]
        + [w_qkv[0, :, PAIR:], w_qkv[1, :, PAIR:], w_qkv[2, :, PAIR:], out_t[:, PAIR:]],
        axis=1,
    ).astype(BF)
    packed, up_part, down_part = after(packed, w_up, w_down)
    down_t = down_part.T
    cut = w_up.shape[1] * 2 // 3
    packed_one = jnp.concatenate([up_part[:, :cut], down_t[:, :cut]], axis=1).astype(BF)
    packed_two = jnp.concatenate([up_part[:, cut:], down_t[:, cut:]], axis=1).astype(BF)
    own_length = lax.dynamic_slice_in_dim(lengths, t_index, 1, 0)
    own_latent = lax.dynamic_slice_in_dim(latent, t_index, 1, 0)
    positions = lax.broadcasted_iota(jnp.int32, (1, rows), 1)
    keep = ((positions < own_length) & (own_latent == 0)).astype(BF).reshape(rows, 1)
    cot = cotangent * keep

    fast = n_dp == 8 and n_tensor == 4
    d_index = lax.axis_index("dp")
    place = jnp.stack([d_index >> 1, d_index & 1, t_index >> 1, t_index & 1]).astype(jnp.int32)

    def gather(piece):
        wide = piece.shape[1]
        full = lax.all_gather(piece, BOTH, axis=0, tiled=False)
        full = full.reshape(n_dp, n_tensor, block, wide)
        if fast:
            return full
        return full.transpose(1, 0, 2, 3).reshape(1, n_tensor, width, wide)

    project_place = place
    def to_inner(b):
        split = b.reshape(b.shape[0], n_tensor, heads, HEAD_DIM)
        return jnp.concatenate(
            [split[:, :, :2].reshape(b.shape[0], -1), split[:, :, 2:].reshape(b.shape[0], -1)],
            axis=1,
        )

    zero = jnp.zeros_like(b_out)
    early = [
        cot,
        place,
        own_length,
        to_inner(b_qv),
        ln1_gain[None],
        ln1_bias[None],
        jnp.stack([b_out, ln2_gain, ln2_bias, b_down, zero, zero, zero, zero]),
        b_up.reshape(n_tensor, 1, width),
    ]
    if fast:
        def grow(array, came):
            return jnp.concatenate([array, came])

        att, one, two = packed[None], packed_one[None], packed_two[None]
        att_came, two_came, one, *early = after(
            exchange(att, flip_near), exchange(two, flip_first), one, *early
        )
        att, two = grow(att, att_came), grow(two, two_came)
        att_came, two_came, one_one = after(
            exchange(att, flip_far), exchange(two, flip_second), exchange(one, flip_ring)
        )
        att, two = grow(att, att_came), grow(two, two_came)
        att_first, att_second, one_two, two_one = after(
            exchange(att, flip_first),
            exchange(att, flip_second),
            exchange(one_one, flip_ring),
            exchange(two, flip_ring),
        )
        halves = [att, att_first, att_second]
        att_both, one_last, *cores = after(
            exchange(att_first, flip_second),
            exchange(one_two, flip_ring),
            *(exchange(half, flip_core) for half in halves),
        )
        sources = [*halves, att_both, *cores, exchange(att_both, flip_core)]
        one = jnp.concatenate([one, one_one, one_two, one_last])
        one_first, two_two = exchange(one, flip_first), exchange(two_one, flip_ring)
    else:
        sources = [gather(packed)]
        sources_one, sources_two = [gather(packed_one)], [gather(packed_two)]

    def from_inner(b):
        cut = n_tensor * PAIR
        first = b[:, :cut].reshape(b.shape[0], n_tensor, 2, HEAD_DIM)
        rest = b[:, cut:].reshape(b.shape[0], n_tensor, heads - 2, HEAD_DIM)
        return jnp.concatenate([first, rest], axis=2).reshape(b.shape[0], width)

    cot, place, own_length, inner_bqv, gain, bias, vecs, up_bias = early
    q, k, v, normed_one, w_all = project(
        place, hidden_in, gain, bias, inner_bqv, sources, n_tensor
    )
    if fast:
        one_first, two_two, q = after(one_first, two_two, q)
        halves = [one, one_first, two, two_one, two_two]
        cores = [exchange(half, flip_core) for half in halves]
        came = [exchange(half, flip_second) for half in halves[:2]]
        came.append(exchange(two_two, flip_ring))
    attended, lse = attend(own_length, q, k, v)
    if fast:
        attended, *moved = after(attended, *came, *cores)
        came, cores = moved[:3], moved[3:]
        cores += [exchange(half, flip_core) for half in came]
        sources_one = [*halves[:2], *came[:2], *cores[:2], *cores[5:7]]
        sources_two = [*halves[2:], came[2], *cores[2:5], cores[7]]
    resid, act, g_b_up, d_resid, d_attended, sums_two, last_out, *g_mlp = feed_forward(
        place, attended, hidden_in, cot, w_all, vecs, up_bias, sources_one, sources_two, fast
    )

    half = len(g_mlp) // 2

    def back(length, first, pairs, wide, so_far):
        return list(
            attend_back(
                place, length, first, pairs, wide, q, k, v, attended, d_attended, lse,
                normed_one, last_out, n_tensor, so_far, fast,
            )
        )

    def vectors(sums_one):
        return jnp.concatenate([sums_one[:4], sums_two[:4], g_b_up.reshape(n_tensor, width)])

    if fast:
        up, down = Scatter(*g_mlp[:half]), Scatter(*g_mlp[half:])
        came_up, came_down = up.step(), down.step()
        hidden_out = hidden_rows(place, act, resid, vecs, sources_one, sources_two)
        came_up, came_down, length, hidden_out = after(
            came_up, came_down, own_length, hidden_out
        )
        up.sent, down.sent = sums(up.want(came_up), down.want(came_down))
        came_up, came_down = up.step(), down.step()
        back_one = back(length, 0, 4, 3 * PAIR, None)
        came_up, length, *back_one = after(came_up, own_length, *back_one)
        (up.sent,) = sums(up.want(came_up))
        came_up = up.step()
        back_two = back(length, 4, 2, 2 * PAIR, back_one[3:])
        came_up, came_down, gain, *back_two = after(came_up, came_down, gain, *back_two)
        rest = Scatter(*back_two[3:])
        came_rest = rest.step()
        up.sent, down.sent = sums(up.want(came_up), down.want(came_down))
        came_rest, up.sent, down.sent = after(came_rest, up.sent, down.sent)
        came_up, came_down = up.step(), down.step()
        (rest.sent,) = sums(rest.want(came_rest))
        came_rest = rest.step()
        parts = [*back_one[:3], *back_two[:3]]
        grad_in, sums_one = input_grad(parts, w_all, hidden_in, d_resid, gain)
        came_rest, came_down, sums_one, grad_in = after(came_rest, came_down, sums_one, grad_in)
        rest.sent, down.sent = sums(rest.want(came_rest), down.want(came_down))
        came_up, rest.sent, down.sent = after(came_up, rest.sent, down.sent)
        came_rest, came_down = rest.step(), down.step()
        (up.sent,) = plain_sums(up.want(came_up))
        came_up = up.step()
        small = vectors(sums_one)
        small = small + exchange(small, flip_core)
        came_small = exchange(small, flip_second)
        small = small + came_small
        came_small = exchange(small, flip_first)
        came_rest, came_down, came_small = after(came_rest, came_down, came_small)
        (rest.sent,) = plain_sums(rest.want(came_rest))
        small = small + came_small
        rest.sent, came_down = after(rest.sent, came_down)
        came_rest, came_small = rest.step(), exchange(small, flip_far)
        (down.sent,) = plain_sums(down.want(came_down))
        came_down = down.step()
        came_rest, came_small, came_up, came_down = after(
            came_rest, came_small, came_up, came_down
        )
        (rest.sent,) = plain_sums(rest.want(came_rest))
        small = small + came_small
        came_rest, came_small = rest.step(), exchange(small, flip_near)
        small = small + came_small
        g_up, g_out, g_down, g_qkv = last_sums(
            [*up.terms, came_up], [*down.terms, came_down], [*rest.terms, came_rest]
        )
    else:
        back_one = back(own_length, 0, 4, 3 * PAIR, None)
        back_two = back(own_length, 4, 2, 2 * PAIR, back_one[3:])
        parts = [*back_one[:3], *back_two[:3]]
        grad_in, sums_one = input_grad(parts, w_all, hidden_in, d_resid, gain)
        hidden_out = hidden_rows(place, act, resid, vecs, sources_one, sources_two)
        small = lax.psum(vectors(sums_one), BOTH)

        def scatter_all(grads):
            wide = grads.shape[-1]
            grads = grads.reshape(n_tensor, n_dp, block, wide).transpose(1, 0, 2, 3)
            flat = grads.reshape(n_dp * n_tensor * block, wide)
            total = lax.psum_scatter(flat, BOTH, scatter_dimension=0, tiled=True)
            return total.astype(F32)

        g_up, g_down, g_rest = (scatter_all(g) for g in (*g_mlp, back_two[3]))
        g_out, g_qkv = split_columns(g_up, g_rest)
        g_out = g_out.T
        g_up = g_up[:, :width]
    g_bqv = from_inner(small[2:4])

    return (
        hidden_out,
        grad_in,
        small[0],
        small[1],
        g_qkv,
        g_bqv,
        g_out,
        small[6],
        small[4],
        small[5],
        g_up,
        small[8:].reshape(-1),
        g_down.T,
        small[7],
    )


def solution(mesh):
    placed = (
        P(BOTH, None),
        P(BOTH, None),
        P("dp"),
        P("dp", None),
        P(),
        P(),
        P(None, "dp", "tensor"),
        P(),
        P("tensor", "dp"),
        P(),
        P(),
        P(),
        P("dp", "tensor"),
        P(),
        P("tensor", "dp"),
        P(),
    )
    return jax.shard_map(
        functools.partial(body, mesh.shape["dp"], mesh.shape["tensor"]),
        mesh=mesh,
        in_specs=placed,
        out_specs=(
            P(BOTH, None),
            P(BOTH, None),
            P(),
            P(),
            P(None, "dp", "tensor"),
            P(),
            P("tensor", "dp"),
            P(),
            P(),
            P(),
            P("dp", "tensor"),
            P(),
            P("tensor", "dp"),
            P(),
        ),
        check_vma=False,
    )
```

profile of v0, /device:TPU:0, one launch (start us, length us, event | category | flops | bytes accessed | tf_op | source)
XLA Modules:
  0.0 290.4 jit_solution(15687781732863716683)
XLA Ops:
  4.0 3.0 %collective-permute-start.1 = (bf16[1,96,512]{2,1,0:T(8,128)(2,1)S(1)}, bf16[1,96,512]{2,1,0:T(8,128)(2,1)S(1)}, u32[]{:S(2)}, u32[]{:S(2)}) collective-permute-start(bf16[1,96,512]{2,1,0:T(8,128)(2,1)S(1)} %pad_maximum_fusion.5), channel_id=1, source_target_pairs={{0,4},{1,3},{2,6},{3,1},{4,0},{5,7},{6,2},{7,5},{8,12},{9,11},{10,... | collective-permute-start | bytes 294920 | tf_op jit(solution)/shard_map/ppermute | solution.py:78
  15.6 2.7 collective-permute-start.2
  20.3 3.7 %collective-permute-done.3 = bf16[2,96,512]{2,1,0:T(8,128)(2,1)S(1)} collective-permute-done((bf16[2,96,512]{2,1,0:T(8,128)(2,1)S(1)}, bf16[2,96,512]{2,1,0:T(8,128)(2,1)S(1)}, u32[]{:S(2)}, u32[]{:S(2)}) %collective-permute-start.3) | collective-permute-done | bytes 196640 | tf_op jit(solution)/shard_map/ppermute | solution.py:78
  24.0 11.2 %collective-permute-done.4 = bf16[1,96,1024]{2,1,0:T(8,128)(2,1)S(1)} collective-permute-done((bf16[1,96,1024]{2,1,0:T(8,128)(2,1)S(1)}, bf16[1,96,1024]{2,1,0:T(8,128)(2,1)S(1)}, u32[]{:S(2)}, u32[]{:S(2)}) %collective-permute-start.4) | collective-permute-done | bytes 196640 | tf_op jit(solution)/shard_map/ppermute | solution.py:78
  38.1 3.1 %collective-permute-start.7 = (bf16[1,96,1024]{2,1,0:T(8,128)(2,1)S(1)}, bf16[1,96,1024]{2,1,0:T(8,128)(2,1)S(1)}, u32[]{:S(2)}, u32[]{:S(2)}) collective-permute-start(bf16[1,96,1024]{2,1,0:T(8,128)(2,1)S(1)} %collective-permute-done.4), channel_id=1, source_target_pairs={{0,8},{1,9},{2,10},{3,11},{4,12},{5,13},{6,14},{7,15},{8,24},{9,25... | collective-permute-start | bytes 589832 | tf_op jit(solution)/shard_map/ppermute | solution.py:78
  41.2 12.6 %collective-permute-done.7 = bf16[1,96,1024]{2,1,0:T(8,128)(2,1)S(1)} collective-permute-done((bf16[1,96,1024]{2,1,0:T(8,128)(2,1)S(1)}, bf16[1,96,1024]{2,1,0:T(8,128)(2,1)S(1)}, u32[]{:S(2)}, u32[]{:S(2)}) %collective-permute-start.7) | collective-permute-done | bytes 196640 | tf_op jit(solution)/shard_map/ppermute | solution.py:78
  57.5 5.2 %collective-permute-done.10 = bf16[1,96,1024]{2,1,0:T(8,128)(2,1)S(1)} collective-permute-done((bf16[1,96,1024]{2,1,0:T(8,128)(2,1)S(1)}, bf16[1,96,1024]{2,1,0:T(8,128)(2,1)S(1)}, u32[]{:S(2)}, u32[]{:S(2)}) %collective-permute-start.10) | collective-permute-done | bytes 196640 | tf_op jit(solution)/shard_map/ppermute | solution.py:78
  69.0 12.1 %project.1 = (bf16[1024,768]{1,0:T(8,128)(2,1)}, bf16[1024,768]{1,0:T(8,128)(2,1)}, bf16[1024,768]{1,0:T(8,128)(2,1)}, bf16[1024,768]{1,0:T(8,128)(2,1)}, bf16[4,768,768]{2,1,0:T(8,128)(2,1)}) custom-call(s32[4]{0:T(128)} %pad_add_fusion.place_ref, bf16[1024,768]{1,0:T(8,128)(2,1)} %refs_7_.1, f32[1,768]{1,0:T(1,128)} %broadcast_in_dim.13.gain_ref.refs_9_, ...), custom_call_target="tpu_custom_call" | custom-call | flops 3623878656 | bytes 12582912 | tf_op jit(solution)/shard_map/project/pallas_call | solution.py:362
  86.0 16.9 %attend.1 = (bf16[1024,768]{1,0:T(8,128)(2,1)}, f32[6,8,1024]{2,1,0:T(8,128)}) custom-call(s32[1]{0:T(128)} %dynamic_slice.6.len_ref, bf16[1024,768]{1,0:T(8,128)(2,1)} %get-tuple-element.154.q_ref, bf16[1024,768]{1,0:T(8,128)(2,1)} %get-tuple-element.155.k_ref, bf16[1024,768]{1,0:T(8,128)(2,1)} %get-tuple-element.156.v_ref), custom_call_target="tpu_custom_call" | custom-call | flops 16000000000 | bytes 6291456 | tf_op jit(solution)/shard_map/attend/pallas_call | solution.py:445
  103.6 3.7 %collective-permute-done.27.refs_15_ = bf16[4,96,512]{2,1,0:T(8,128)(2,1)} collective-permute-done((bf16[4,96,512]{2,1,0:T(8,128)(2,1)}, bf16[4,96,512]{2,1,0:T(8,128)(2,1)}, u32[]{:S(2)}, u32[]{:S(2)}) %collective-permute-start.27) | collective-permute-done | bytes 393248 | tf_op jit(solution)/shard_map/ppermute | solution.py:78
  107.3 45.8 %feed_forward.1 = (f32[1024,768]{1,0:T(8,128)}, bf16[1024,3072]{1,0:T(8,128)(2,1)}, f32[4,1,768]{2,1,0:T(1,128)}, f32[1024,768]{1,0:T(8,128)}, bf16[1024,768]{1,...) custom-call(s32[4]{0:T(128)} %pad_add_fusion.place_ref, ...), custom_call_target="tpu_custom_call" | custom-call | flops 40000000000 | bytes 40000000 | tf_op jit(solution)/shard_map/feed_forward/pallas_call | solution.py:750
  153.7 11.8 %hidden_rows.1 = bf16[1024,768]{1,0:T(8,128)(2,1)} custom-call(s32[4]{0:T(128)} %pad_add_fusion.place_ref, bf16[1024,3072]{1,0:T(8,128)(2,1)} %get-tuple-element.175.act_ref, f32[1024,768]{1,0:T(8,128)} %get-tuple-element.176.resid_ref, f32[8,768]{1,0:T(8,128)} %stack.43.vec_ref, bf16[4,96,1024]{2,1,0:T(8,128)(2,1)} %constant_dynamic-update-slice_fusion.refs_0_, ...), custom_call_target="tpu_custom_call" | custom-call | flops 5000000000 | bytes 12000000 | tf_op jit(solution)/shard_map/hidden_rows/pallas_call | solution.py:835
  165.5 4.0 %sums.5 = (bf16[8,96,896]{2,1,0:T(8,128)(2,1)}, bf16[8,96,768]{2,1,0:T(8,128)(2,1)}) custom-call(bf16[16,96,896]{2,1,0:T(8,128)(2,1)} %get-tuple-element.178.refs_0_, bf16[16,96,896]{2,1,0:T(8,128)(2,1)} %collective-permute-done.28.refs_1_, bf16[16,96,768]{2,1,0:T(8,128)(2,1)} %get-tuple-element.180.refs_2_.refs_4_.refs_3_.refs_6_, ...), custom_call_target="tpu_custom_call" | custom-call | flops 1000000 | bytes 8000000 | tf_op jit(solution)/shard_map/sums/pallas_call | solution.py:145
  171.7 24.6 %attend_back.2 = (bf16[1024,512]{1,0:T(8,128)(2,1)}, bf16[1024,512]{1,0:T(8,128)(2,1)}, bf16[1024,512]{1,0:T(8,128)(2,1)}, bf16[16,96,640]{2,1,0:T(8,128)(2,1)}, bf16[16,96,640]{2,1,0:T(8,128)(2,1)}) custom-call(s32[1]{0:T(128)} %dynamic_slice.6.len_ref, s32[4]{0:T(128)} %pad_add_fusion.place_ref, bf16[1024,768]{1,0:T(8,128)(2,1)} %get-tuple-element.154.q_ref, ...), custom_call_target="tpu_custom_call" | custom-call | flops 12000000000 | bytes 20000000 | tf_op jit(solution)/shard_map/attend_back/pallas_call | solution.py:577
  199.1 15.4 %attend_back.3 = (bf16[1024,256]{1,0:T(8,128)(2,1)}, bf16[1024,256]{1,0:T(8,128)(2,1)}, bf16[1024,256]{1,0:T(8,128)(2,1)}, bf16[16,96,640]{2,1,0:T(8,128)(2,1)}, bf16[16,96,640]{2,1,0:T(8,128)(2,1)}) custom-call(s32[1]{0:T(128)} %dynamic_slice.6.len_ref, s32[4]{0:T(128)} %pad_add_fusion.place_ref, ...), custom_call_target="tpu_custom_call", output_to_operand_aliasing={{3}: (10, {}), {4}: (11, {})} | custom-call | flops 6000000000 | bytes 10000000 | tf_op jit(solution)/shard_map/attend_back/pallas_call | solution.py:577
  214.6 2.9 %sums.7 = (bf16[2,96,896]{2,1,0:T(8,128)(2,1)}, bf16[4,96,768]{2,1,0:T(8,128)(2,1)}) custom-call(bf16[16,96,896]{2,1,0:T(8,128)(2,1)} %get-tuple-element.178.refs_0_, bf16[16,96,896]{2,1,0:T(8,128)(2,1)} %collective-permute-done.28.refs_1_, bf16[8,96,896]{2,1,0:T(8,128)(2,1)} %collective-permute-done.30.refs_2_, ...), custom_call_target="tpu_custom_call" | custom-call | flops 1000000 | bytes 8000000 | tf_op jit(solution)/shard_map/sums/pallas_call | solution.py:145
  225.3 10.1 %input_grad.1 = (f32[1024,768]{1,0:T(8,128)}, f32[8,768]{1,0:T(8,128)}) custom-call(bf16[1024,512]{1,0:T(8,128)(2,1)} %get-tuple-element.211.refs_0_, bf16[1024,512]{1,0:T(8,128)(2,1)} %get-tuple-element.212.refs_1_, bf16[1024,512]{1,0:T(8,128)(2,1)} %get-tuple-element.213.refs_2_, bf16[1024,256]{1,0:T(8,128)(2,1)} %get-tuple-element.214.refs_3_, ...), custom_call_target="tpu_custom_call" | custom-call | flops 3623878656 | bytes 12582912 | tf_op jit(solution)/shard_map/input_grad/pallas_call | solution.py:884
  235.4 4.0 %collective-permute-done.35.refs_6_.refs_9_ = bf16[4,96,768]{2,1,0:T(8,128)(2,1)} collective-permute-done((bf16[4,96,768]{2,1,0:T(8,128)(2,1)}, bf16[4,96,768]{2,1,0:T(8,128)(2,1)}, u32[]{:S(2)}, u32[]{:S(2)}) %collective-permute-start.35) | collective-permute-done | bytes 589856 | tf_op jit(solution)/shard_map/ppermute | solution.py:78
  242.8 2.7 sums.9
  249.6 3.6 %collective-permute-done.37 = f32[12,768]{1,0:T(8,128)S(1)} collective-permute-done((f32[12,768]{1,0:T(8,128)S(1)}, f32[12,768]{1,0:T(8,128)S(1)}, u32[]{:S(2)}, u32[]{:S(2)}) %collective-permute-start.37) | collective-permute-done | bytes 36896 | tf_op jit(solution)/shard_map/ppermute | solution.py:78
  257.4 5.1 %collective-permute-done.40.refs_10_ = bf16[2,96,768]{2,1,0:T(8,128)(2,1)S(1)} collective-permute-done((bf16[2,96,768]{2,1,0:T(8,128)(2,1)}, bf16[2,96,768]{2,1,0:T(8,128)(2,1)S(1)}, u32[]{:S(2)}, u32[]{:S(2)}) %collective-permute-start.40) | collective-permute-done | bytes 294944 | tf_op jit(solution)/shard_map/ppermute | solution.py:78
  265.4 2.6 collective-permute-start.45
  268.5 10.8 %collective-permute-done.43 = f32[12,768]{1,0:T(8,128)S(1)} collective-permute-done((f32[12,768]{1,0:T(8,128)S(1)}, f32[12,768]{1,0:T(8,128)S(1)}, u32[]{:S(2)}, u32[]{:S(2)}) %collective-permute-start.43) | collective-permute-done | bytes 36896 | tf_op jit(solution)/shard_map/ppermute | solution.py:78
  287.4 2.8 last_sums.1
  (198 shorter events, 68.3 us)
Async XLA Ops:
  15.6 19.6 %collective-permute-start.2 = (bf16[2,96,768]{2,1,0:T(8,128)(2,1)S(1)}, bf16[2,96,768]{2,1,0:T(8,128)(2,1)S(1)}, u32[]{:S(2)}, u32[]{:S(2)}) collective-permute-start(bf16[2,96,768]{2,1,0:T(8,128)(2,1)S(1)} %pad_maximum_fusion.2), channel_id=1, source_target_pairs={{0,16},{1,17},{2,18},{3,19},{4,20},{5,21},{6,22},{7,23},{8,24},{9,... | collective-permute-start | bytes 884744 | tf_op jit(solution)/shard_map/ppermute | solution.py:78
  19.8 15.3 %collective-permute-start.4 = (bf16[1,96,1024]{2,1,0:T(8,128)(2,1)S(1)}, bf16[1,96,1024]{2,1,0:T(8,128)(2,1)S(1)}, u32[]{:S(2)}, u32[]{:S(2)}) collective-permute-start(bf16[1,96,1024]{2,1,0:T(8,128)(2,1)S(1)} %pad_maximum_fusion.3), channel_id=1, source_target_pairs={{0,8},{1,9},{2,10},{3,11},{4,12},{5,13},{6,14},{7,15},{8,24},{9,25... | collective-permute-start | bytes 589832 | tf_op jit(solution)/shard_map/ppermute | solution.py:78
  35.2 18.7 %collective-permute-start.6 = (bf16[4,96,768]{2,1,0:T(8,128)(2,1)S(1)}, bf16[4,96,768]{2,1,0:T(8,128)(2,1)S(1)}, u32[]{:S(2)}, u32[]{:S(2)}) collective-permute-start(bf16[4,96,768]{2,1,0:T(8,128)(2,1)S(1)} %pad_maximum_fusion.refs_0_), channel_id=1, source_target_pairs={{0,2},{1,5},{2,0},{3,7},{4,6},{5,1},{6,4},{7,3},{8,10},{9,13},{10,... | collective-permute-start | bytes 1769480 | tf_op jit(solution)/shard_map/ppermute | solution.py:78
  35.8 18.1 %collective-permute-start.5 = (bf16[4,96,768]{2,1,0:T(8,128)(2,1)S(1)}, bf16[4,96,768]{2,1,0:T(8,128)(2,1)S(1)}, u32[]{:S(2)}, u32[]{:S(2)}) collective-permute-start(bf16[4,96,768]{2,1,0:T(8,128)(2,1)S(1)} %pad_maximum_fusion.refs_0_), channel_id=1, source_target_pairs={{0,4},{1,3},{2,6},{3,1},{4,0},{5,7},{6,2},{7,5},{8,12},{9,11},{10,... | collective-permute-start | bytes 1769480 | tf_op jit(solution)/shard_map/ppermute | solution.py:78
  38.1 15.8 %collective-permute-start.8 = (bf16[4,96,512]{2,1,0:T(8,128)(2,1)}, bf16[4,96,512]{2,1,0:T(8,128)(2,1)}, u32[]{:S(2)}, u32[]{:S(2)}) collective-permute-start(bf16[4,96,512]{2,1,0:T(8,128)(2,1)} %pad_maximum_fusion.1.refs_8_), channel_id=1, source_target_pairs={{0,8},{1,9},{2,10},{3,11},{4,12},{5,13},{6,14},{7,15},{8,24},{9,25... | collective-permute-start | bytes 1179656 | tf_op jit(solution)/shard_map/ppermute | solution.py:78
  38.1 15.8 %collective-permute-start.7 = (bf16[1,96,1024]{2,1,0:T(8,128)(2,1)S(1)}, bf16[1,96,1024]{2,1,0:T(8,128)(2,1)S(1)}, u32[]{:S(2)}, u32[]{:S(2)}) collective-permute-start(bf16[1,96,1024]{2,1,0:T(8,128)(2,1)S(1)} %collective-permute-done.4), channel_id=1, source_target_pairs={{0,8},{1,9},{2,10},{3,11},{4,12},{5,13},{6,14},{7,15},{8,24},{9,25... | collective-permute-start | bytes 589832 | tf_op jit(solution)/shard_map/ppermute | solution.py:78
  41.2 16.2 %collective-permute-start.11 = (bf16[4,96,768]{2,1,0:T(8,128)(2,1)S(1)}, bf16[4,96,768]{2,1,0:T(8,128)(2,1)S(1)}, u32[]{:S(2)}, u32[]{:S(2)}) collective-permute-start(bf16[4,96,768]{2,1,0:T(8,128)(2,1)S(1)} %pad_maximum_fusion.refs_0_), channel_id=1, source_target_pairs={{0,1},{1,0},{2,3},{3,2},{4,5},{5,4},{6,7},{7,6},{8,9},{9,8},{10,11... | collective-permute-start | bytes 1769480 | tf_op jit(solution)/shard_map/ppermute | solution.py:78
  65.8 15.9 %collective-permute-start.14 = (bf16[4,96,1024]{2,1,0:T(8,128)(2,1)}, bf16[4,96,1024]{2,1,0:T(8,128)(2,1)}, u32[]{:S(2)}, u32[]{:S(2)}) collective-permute-start(bf16[4,96,1024]{2,1,0:T(8,128)(2,1)} %constant_dynamic-update-slice_fusion.refs_0_), channel_id=1, source_target_pairs={{0,4},{1,3},{2,6},{3,1},{4,0},{5,7},{6,2},{7,5},{8,12},{9,11},{10,... | collective-permute-start | bytes 2359304 | tf_op jit(solution)/shard_map/ppermute | solution.py:78
  66.3 18.0 %collective-permute-start.20 = (bf16[4,96,1024]{2,1,0:T(8,128)(2,1)}, bf16[4,96,1024]{2,1,0:T(8,128)(2,1)}, u32[]{:S(2)}, u32[]{:S(2)}) collective-permute-start(bf16[4,96,1024]{2,1,0:T(8,128)(2,1)} %constant_dynamic-update-slice_fusion.refs_0_), channel_id=1, source_target_pairs={{0,1},{1,0},{2,3},{3,2},{4,5},{5,4},{6,7},{7,6},{8,9},{9,8},{10,11... | collective-permute-start | bytes 2359304 | tf_op jit(solution)/shard_map/ppermute | solution.py:78
  68.5 15.7 %collective-permute-start.23 = (bf16[4,96,512]{2,1,0:T(8,128)(2,1)}, bf16[4,96,512]{2,1,0:T(8,128)(2,1)}, u32[]{:S(2)}, u32[]{:S(2)}) collective-permute-start(bf16[4,96,512]{2,1,0:T(8,128)(2,1)} %collective-permute-done.8.refs_9_), channel_id=1, source_target_pairs={{0,1},{1,0},{2,3},{3,2},{4,5},{5,4},{6,7},{7,6},{8,9},{9,8},{10,11... | collective-permute-start | bytes 1179656 | tf_op jit(solution)/shard_map/ppermute | solution.py:78
  81.1 21.8 %collective-permute-start.17 = (bf16[4,96,1024]{2,1,0:T(8,128)(2,1)}, bf16[4,96,1024]{2,1,0:T(8,128)(2,1)}, u32[]{:S(2)}, u32[]{:S(2)}) collective-permute-start(bf16[4,96,1024]{2,1,0:T(8,128)(2,1)} %constant_dynamic-update-slice_fusion.refs_0_), channel_id=1, source_target_pairs={{0,2},{1,5},{2,0},{3,7},{4,6},{5,1},{6,4},{7,3},{8,10},{9,13},{10,... | collective-permute-start | bytes 2359304 | tf_op jit(solution)/shard_map/ppermute | solution.py:78
  81.7 21.2 %collective-permute-start.24 = (bf16[4,96,512]{2,1,0:T(8,128)(2,1)}, bf16[4,96,512]{2,1,0:T(8,128)(2,1)}, u32[]{:S(2)}, u32[]{:S(2)}) collective-permute-start(bf16[4,96,512]{2,1,0:T(8,128)(2,1)} %collective-permute-done.15.refs_10_), channel_id=1, source_target_pairs={{0,1},{1,0},{2,3},{3,2},{4,5},{5,4},{6,7},{7,6},{8,9},{9,8},{10,11... | collective-permute-start | bytes 1179656 | tf_op jit(solution)/shard_map/ppermute | solution.py:78
  81.7 21.2 %collective-permute-start.19 = (bf16[4,96,512]{2,1,0:T(8,128)(2,1)}, bf16[4,96,512]{2,1,0:T(8,128)(2,1)}, u32[]{:S(2)}, u32[]{:S(2)}) collective-permute-start(bf16[4,96,512]{2,1,0:T(8,128)(2,1)} %collective-permute-done.15.refs_10_), channel_id=1, source_target_pairs={{0,8},{1,9},{2,10},{3,11},{4,12},{5,13},{6,14},{7,15},{8,24},{9,25... | collective-permute-start | bytes 1179656 | tf_op jit(solution)/shard_map/ppermute | solution.py:78
  84.3 18.6 %collective-permute-start.21 = (bf16[4,96,1024]{2,1,0:T(8,128)(2,1)}, bf16[4,96,1024]{2,1,0:T(8,128)(2,1)}, u32[]{:S(2)}, u32[]{:S(2)}) collective-permute-start(bf16[4,96,1024]{2,1,0:T(8,128)(2,1)} %collective-permute-done.14.refs_1_), channel_id=1, source_target_pairs={{0,1},{1,0},{2,3},{3,2},{4,5},{5,4},{6,7},{7,6},{8,9},{9,8},{10,11... | collective-permute-start | bytes 2359304 | tf_op jit(solution)/shard_map/ppermute | solution.py:78
  84.3 18.6 %collective-permute-start.18 = (bf16[4,96,1024]{2,1,0:T(8,128)(2,1)}, bf16[4,96,1024]{2,1,0:T(8,128)(2,1)}, u32[]{:S(2)}, u32[]{:S(2)}) collective-permute-start(bf16[4,96,1024]{2,1,0:T(8,128)(2,1)} %collective-permute-done.14.refs_1_), channel_id=1, source_target_pairs={{0,2},{1,5},{2,0},{3,7},{4,6},{5,1},{6,4},{7,3},{8,10},{9,13},{10,... | collective-permute-start | bytes 2359304 | tf_op jit(solution)/shard_map/ppermute | solution.py:78
  169.6 26.7 %collective-permute-start.30 = (bf16[8,96,896]{2,1,0:T(8,128)(2,1)}, bf16[8,96,896]{2,1,0:T(8,128)(2,1)}, u32[]{:S(2)}, u32[]{:S(2)}) collective-permute-start(bf16[8,96,896]{2,1,0:T(8,128)(2,1)} %get-tuple-element.182), channel_id=1, source_target_pairs={{0,2},{1,5},{2,0},{3,7},{4,6},{5,1},{6,4},{7,3},{8,10},{9,13},{10,... | collective-permute-start | bytes 4128776 | tf_op jit(solution)/shard_map/ppermute | solution.py:78
  170.0 44.5 %collective-permute-start.32 = (bf16[8,96,768]{2,1,0:T(8,128)(2,1)}, bf16[8,96,768]{2,1,0:T(8,128)(2,1)}, u32[]{:S(2)}, u32[]{:S(2)}) collective-permute-start(bf16[8,96,768]{2,1,0:T(8,128)(2,1)} %get-tuple-element.194), channel_id=1, source_target_pairs={{0,2},{1,5},{2,0},{3,7},{4,6},{5,1},{6,4},{7,3},{8,10},{9,13},{10,... | collective-permute-start | bytes 3538952 | tf_op jit(solution)/shard_map/ppermute | solution.py:78
  198.7 15.8 %collective-permute-start.31 = (bf16[4,96,896]{2,1,0:T(8,128)(2,1)}, bf16[4,96,896]{2,1,0:T(8,128)(2,1)}, u32[]{:S(2)}, u32[]{:S(2)}) collective-permute-start(bf16[4,96,896]{2,1,0:T(8,128)(2,1)} %sums.6), channel_id=1, source_target_pairs={{0,4},{1,3},{2,6},{3,1},{4,0},{5,7},{6,2},{7,5},{8,12},{9,11},{10,... | collective-permute-start | bytes 2064392 | tf_op jit(solution)/shard_map/ppermute | solution.py:78
  221.2 20.8 %collective-permute-start.34 = (bf16[8,96,640]{2,1,0:T(8,128)(2,1)}, bf16[8,96,640]{2,1,0:T(8,128)(2,1)}, u32[]{:S(2)}, u32[]{:S(2)}) collective-permute-start(bf16[8,96,640]{2,1,0:T(8,128)(2,1)} %sums.8), channel_id=1, source_target_pairs={{0,2},{1,5},{2,0},{3,7},{4,6},{5,1},{6,4},{7,3},{8,10},{9,13},{10,... | collective-permute-start | bytes 2949128 | tf_op jit(solution)/shard_map/ppermute | solution.py:78
  222.8 16.6 %collective-permute-start.35 = (bf16[4,96,768]{2,1,0:T(8,128)(2,1)}, bf16[4,96,768]{2,1,0:T(8,128)(2,1)}, u32[]{:S(2)}, u32[]{:S(2)}) collective-permute-start(bf16[4,96,768]{2,1,0:T(8,128)(2,1)} %get-tuple-element.210), channel_id=1, source_target_pairs={{0,4},{1,3},{2,6},{3,1},{4,0},{5,7},{6,2},{7,5},{8,12},{9,11},{10,... | collective-permute-start | bytes 1769480 | tf_op jit(solution)/shard_map/ppermute | solution.py:78
  223.3 22.2 %collective-permute-start.38 = (bf16[2,96,896]{2,1,0:T(8,128)(2,1)}, bf16[2,96,896]{2,1,0:T(8,128)(2,1)}, u32[]{:S(2)}, u32[]{:S(2)}) collective-permute-start(bf16[2,96,896]{2,1,0:T(8,128)(2,1)} %get-tuple-element.225), channel_id=1, source_target_pairs={{0,16},{1,17},{2,18},{3,19},{4,20},{5,21},{6,22},{7,23},{8,24},{9,... | collective-permute-start | bytes 1032200 | tf_op jit(solution)/shard_map/ppermute | solution.py:78
  245.5 17.0 %collective-permute-start.40 = (bf16[2,96,768]{2,1,0:T(8,128)(2,1)}, bf16[2,96,768]{2,1,0:T(8,128)(2,1)S(1)}, u32[]{:S(2)}, u32[]{:S(2)}) collective-permute-start(bf16[2,96,768]{2,1,0:T(8,128)(2,1)} %get-tuple-element.231), channel_id=1, source_target_pairs={{0,16},{1,17},{2,18},{3,19},{4,20},{5,21},{6,22},{7,23},{8,24},{9,... | collective-permute-start | bytes 884744 | tf_op jit(solution)/shard_map/ppermute | solution.py:78
  247.6 15.0 %collective-permute-start.39 = (bf16[4,96,640]{2,1,0:T(8,128)(2,1)}, bf16[4,96,640]{2,1,0:T(8,128)(2,1)S(1)}, u32[]{:S(2)}, u32[]{:S(2)}) collective-permute-start(bf16[4,96,640]{2,1,0:T(8,128)(2,1)} %get-tuple-element.230), channel_id=1, source_target_pairs={{0,4},{1,3},{2,6},{3,1},{4,0},{5,7},{6,2},{7,5},{8,12},{9,11},{10,... | collective-permute-start | bytes 1474568 | tf_op jit(solution)/shard_map/ppermute | solution.py:78
  264.1 15.2 %collective-permute-start.42 = (bf16[2,96,640]{2,1,0:T(8,128)(2,1)S(1)}, bf16[2,96,640]{2,1,0:T(8,128)(2,1)S(1)}, u32[]{:S(2)}, u32[]{:S(2)}) collective-permute-start(bf16[2,96,640]{2,1,0:T(8,128)(2,1)S(1)} %add_convert_fusion), channel_id=1, source_target_pairs={{0,16},{1,17},{2,18},{3,19},{4,20},{5,21},{6,22},{7,23},{8,24},{9,... | collective-permute-start | bytes 737288 | tf_op jit(solution)/shard_map/ppermute | solution.py:78
  (50 other events, 391.5 us)
where the time goes:
time: 291 us; the launch traced here: 290 us
  Pallas kernels  154 us (53%)
  waiting for transfers between devices  68.1 us (23%)
  starting transfers between devices  42.9 us (15%)
  other arithmetic  12.2 us (4%)
  local copies, waits for them, and re-layouts  11.9 us (4%)
    ppermute x48, waiting for transfers between devices, exchange(): return lax.ppermute(array, BOTH, pairs)  68.1 us
    pallas_call x1, Pallas kernels, feed_forward(): pl.pallas_call(functools.partial(feed_kernel, counts), grid_spec=pltpu.Pr...  45.8 us
    ppermute x48, starting transfers between devices, exchange(): return lax.ppermute(array, BOTH, pairs)  42.9 us
    pallas_call x2, Pallas kernels, attend_back(): pl.pallas_call(functools.partial(attend_back_kernel, first, len(grads), b...  40 us
    pallas_call x1, Pallas kernels, attend(): pl.pallas_call(attend_kernel, grid_spec=pltpu.PrefetchScalarGridSpec(num_...  16.9 us
    pallas_call x5, Pallas kernels, sums(): pl.pallas_call(functools.partial(sums_kernel, plan), in_specs=[ANY_SPEC]...  14.4 us
    pallas_call x1, Pallas kernels, project(): pl.pallas_call(functools.partial(qkv_kernel, len(sources)), grid_spec=plt...  12.1 us
    pallas_call x1, Pallas kernels, hidden_rows(): pl.pallas_call(functools.partial(hidden_kernel, counts), grid_spec=pltpu....  11.8 us
  transfers between devices with their start and end apart: 48, of which 15 were waited for; matrix products, arithmetic and copies ran while one was open for 6% of the time, Pallas kernels for 34%

commit v1 on v0

--- a/solution.py
+++ b/solution.py
@@ -938,11 +938,6 @@
     cut = w_up.shape[1] * 2 // 3
     packed_one = jnp.concatenate([up_part[:, :cut], down_t[:, :cut]], axis=1).astype(BF)
     packed_two = jnp.concatenate([up_part[:, cut:], down_t[:, cut:]], axis=1).astype(BF)
-    own_length = lax.dynamic_slice_in_dim(lengths, t_index, 1, 0)
-    own_latent = lax.dynamic_slice_in_dim(latent, t_index, 1, 0)
-    positions = lax.broadcasted_iota(jnp.int32, (1, rows), 1)
-    keep = ((positions < own_length) & (own_latent == 0)).astype(BF).reshape(rows, 1)
-    cot = cotangent * keep
 
     fast = n_dp == 8 and n_tensor == 4
     d_index = lax.axis_index("dp")
@@ -964,28 +959,38 @@
             axis=1,
         )
 
-    zero = jnp.zeros_like(b_out)
-    early = [
-        cot,
-        place,
-        own_length,
-        to_inner(b_qv),
-        ln1_gain[None],
-        ln1_bias[None],
-        jnp.stack([b_out, ln2_gain, ln2_bias, b_down, zero, zero, zero, zero]),
-        b_up.reshape(n_tensor, 1, width),
-    ]
+    raw = [cotangent, lengths, latent, b_qv, ln1_gain, ln1_bias, b_out, ln2_gain, ln2_bias, b_down, b_up]
+
+    def small_operands(
+        cotangent, lengths, latent, b_qv, ln1_gain, ln1_bias, b_out, ln2_gain, ln2_bias, b_down, b_up
+    ):
+        own_length = lax.dynamic_slice_in_dim(lengths, t_index, 1, 0)
+        own_latent = lax.dynamic_slice_in_dim(latent, t_index, 1, 0)
+        positions = lax.broadcasted_iota(jnp.int32, (1, rows), 1)
+        keep = ((positions < own_length) & (own_latent == 0)).astype(BF).reshape(rows, 1)
+        cot = cotangent * keep
+        zero = jnp.zeros_like(b_out)
+        return [
+            cot,
+            place,
+            own_length,
+            to_inner(b_qv),
+            ln1_gain[None],
+            ln1_bias[None],
+            jnp.stack([b_out, ln2_gain, ln2_bias, b_down, zero, zero, zero, zero]),
+            b_up.reshape(n_tensor, 1, width),
+        ]
     if fast:
         def grow(array, came):
             return jnp.concatenate([array, came])
 
         att, one, two = packed[None], packed_one[None], packed_two[None]
-        att_came, two_came, one, *early = after(
-            exchange(att, flip_near), exchange(two, flip_first), one, *early
-        )
-        att, two = grow(att, att_came), grow(two, two_came)
-        att_came, two_came, one_one = after(
-            exchange(att, flip_far), exchange(two, flip_second), exchange(one, flip_ring)
+        att_came, two, one, *raw = after(exchange(att, flip_near), two, one, *raw)
+        early = small_operands(*raw)
+        att = grow(att, att_came)
+        two = grow(two, exchange(two, flip_first))
+        att_came, two_came, one_one, *early = after(
+            exchange(att, flip_far), exchange(two, flip_second), exchange(one, flip_ring), *early
         )
         att, two = grow(att, att_came), grow(two, two_came)
         att_first, att_second, one_two, two_one = after(
@@ -1004,6 +1009,7 @@
         one = jnp.concatenate([one, one_one, one_two, one_last])
         one_first, two_two = exchange(one, flip_first), exchange(two_one, flip_ring)
     else:
+        early = small_operands(*raw)
         sources = [gather(packed)]
         sources_one, sources_two = [gather(packed_one)], [gather(packed_two)]
 

time: 291 us -> 289 us (level)
  waiting for transfers between devices: 68.1 us -> 63.1 us
    ppermute x48, waiting for transfers between devices: 68.1 us -> 63.1 us  [exchange(): return lax.ppermute(array, BOTH, pairs)]
    unnamed x57 -> x59, local copies, waits for them, and re-layouts: 5.44 us -> 6.71 us
  transfers between devices with their start and end apart: 48 -> 48, of which waited for: 15 -> 16; matrix products, arithmetic and copies ran while one was open for 6% -> 7% of each run, Pallas kernels for 34% -> 34%
where the time goes in v1:
time: 289 us; the launch traced here: 288 us
  Pallas kernels  154 us (53%)
  waiting for transfers between devices  63.1 us (22%)
  starting transfers between devices  43.8 us (15%)
  local copies, waits for them, and re-layouts  13.8 us (5%)
  other arithmetic  11.5 us (4%)
    ppermute x48, waiting for transfers between devices, exchange(): return lax.ppermute(array, BOTH, pairs)  63.1 us
    pallas_call x1, Pallas kernels, feed_forward(): pl.pallas_call(functools.partial(feed_kernel, counts), grid_spec=pltpu.Pr...  45.9 us
    ppermute x48, starting transfers between devices, exchange(): return lax.ppermute(array, BOTH, pairs)  43.8 us
    pallas_call x2, Pallas kernels, attend_back(): pl.pallas_call(functools.partial(attend_back_kernel, first, len(grads), b...  39.9 us
    pallas_call x1, Pallas kernels, attend(): pl.pallas_call(attend_kernel, grid_spec=pltpu.PrefetchScalarGridSpec(num_...  16.8 us
    pallas_call x5, Pallas kernels, sums(): pl.pallas_call(functools.partial(sums_kernel, plan), in_specs=[ANY_SPEC]...  14.4 us
    pallas_call x1, Pallas kernels, project(): pl.pallas_call(functools.partial(qkv_kernel, len(sources)), grid_spec=plt...  12.1 us
    pallas_call x1, Pallas kernels, hidden_rows(): pl.pallas_call(functools.partial(hidden_kernel, counts), grid_spec=pltpu....  11.8 us
  transfers between devices with their start and end apart: 48, of which 16 were waited for; matrix products, arithmetic and copies ran while one was open for 7% of the time, Pallas kernels for 34%

profile of v1, /device:TPU:0, one launch (start us, length us, event | category | flops | bytes accessed | tf_op | source)
XLA Modules:
  0.0 287.6 jit_solution(10137153464924982244)
XLA Ops:
  3.1 3.1 %collective-permute-start = (bf16[1,96,768]{2,1,0:T(8,128)(2,1)S(1)}, bf16[1,96,768]{2,1,0:T(8,128)(2,1)S(1)}, u32[]{:S(2)}, u32[]{:S(2)}) collective-permute-start(bf16[1,96,768]{2,1,0:T(8,128)(2,1)S(1)} %bitcast.37), channel_id=1, source_target_pairs={{0,8},{1,9},{2,10},{3,11},{4,12},{5,13},{6,14},{7,15},{8,0},{9,1},... | collective-permute-start | bytes 442376 | tf_op jit(solution)/shard_map/ppermute | solution.py:78
  23.1 5.1 %collective-permute-done.4 = bf16[1,96,1024]{2,1,0:T(8,128)(2,1)S(1)} collective-permute-done((bf16[1,96,1024]{2,1,0:T(8,128)(2,1)S(1)}, bf16[1,96,1024]{2,1,0:T(8,128)(2,1)S(1)}, u32[]{:S(2)}, u32[]{:S(2)}) %collective-permute-start.4) | collective-permute-done | bytes 196640 | tf_op jit(solution)/shard_map/ppermute | solution.py:78
  28.2 4.0 %collective-permute-done.1 = bf16[2,96,768]{2,1,0:T(8,128)(2,1)S(1)} collective-permute-done((bf16[2,96,768]{2,1,0:T(8,128)(2,1)S(1)}, bf16[2,96,768]{2,1,0:T(8,128)(2,1)S(1)}, u32[]{:S(2)}, u32[]{:S(2)}) %collective-permute-start.1) | collective-permute-done | bytes 294944 | tf_op jit(solution)/shard_map/ppermute | solution.py:78
  36.5 3.4 %collective-permute-start.7 = (bf16[1,96,1024]{2,1,0:T(8,128)(2,1)S(1)}, bf16[1,96,1024]{2,1,0:T(8,128)(2,1)S(1)}, u32[]{:S(2)}, u32[]{:S(2)}) collective-permute-start(bf16[1,96,1024]{2,1,0:T(8,128)(2,1)S(1)} %collective-permute-done.4), channel_id=1, source_target_pairs={{0,8},{1,9},{2,10},{3,11},{4,12},{5,13},{6,14},{7,15},{8,24},{9,25... | collective-permute-start | bytes 589832 | tf_op jit(solution)/shard_map/ppermute | solution.py:78
  39.9 10.3 %collective-permute-done.7 = bf16[1,96,1024]{2,1,0:T(8,128)(2,1)S(1)} collective-permute-done((bf16[1,96,1024]{2,1,0:T(8,128)(2,1)S(1)}, bf16[1,96,1024]{2,1,0:T(8,128)(2,1)S(1)}, u32[]{:S(2)}, u32[]{:S(2)}) %collective-permute-start.7) | collective-permute-done | bytes 196640 | tf_op jit(solution)/shard_map/ppermute | solution.py:78
  54.6 4.6 %collective-permute-done.10 = bf16[1,96,1024]{2,1,0:T(8,128)(2,1)S(1)} collective-permute-done((bf16[1,96,1024]{2,1,0:T(8,128)(2,1)S(1)}, bf16[1,96,1024]{2,1,0:T(8,128)(2,1)S(1)}, u32[]{:S(2)}, u32[]{:S(2)}) %collective-permute-start.10) | collective-permute-done | bytes 196640 | tf_op jit(solution)/shard_map/ppermute | solution.py:78
  66.0 12.1 %project.1 = (bf16[1024,768]{1,0:T(8,128)(2,1)}, bf16[1024,768]{1,0:T(8,128)(2,1)}, bf16[1024,768]{1,0:T(8,128)(2,1)}, bf16[1024,768]{1,0:T(8,128)(2,1)}, bf16[4,768,768]{2,1,0:T(8,128)(2,1)}) custom-call(s32[4]{0:T(128)} %pad_add_fusion.place_ref, bf16[1024,768]{1,0:T(8,128)(2,1)} %refs_7_.1, f32[1,768]{1,0:T(1,128)} %broadcast_in_dim.13.gain_ref.refs_9_, ...), custom_call_target="tpu_custom_call" | custom-call | flops 3623878656 | bytes 12582912 | tf_op jit(solution)/shard_map/project/pallas_call | solution.py:362
  78.6 3.6 %collective-permute-start.19 = (bf16[4,96,512]{2,1,0:T(8,128)(2,1)}, bf16[4,96,512]{2,1,0:T(8,128)(2,1)}, u32[]{:S(2)}, u32[]{:S(2)}) collective-permute-start(bf16[4,96,512]{2,1,0:T(8,128)(2,1)} %collective-permute-done.15.refs_10_), channel_id=1, source_target_pairs={{0,8},{1,9},{2,10},{3,11},{4,12},{5,13},{6,14},{7,15},{8,24},{9,25... | collective-permute-start | bytes 1179656 | tf_op jit(solution)/shard_map/ppermute | solution.py:78
  84.0 16.8 %attend.1 = (bf16[1024,768]{1,0:T(8,128)(2,1)}, f32[6,8,1024]{2,1,0:T(8,128)}) custom-call(s32[1]{0:T(128)} %dynamic_slice.6.len_ref, bf16[1024,768]{1,0:T(8,128)(2,1)} %get-tuple-element.176.q_ref, bf16[1024,768]{1,0:T(8,128)(2,1)} %get-tuple-element.177.k_ref, bf16[1024,768]{1,0:T(8,128)(2,1)} %get-tuple-element.178.v_ref), custom_call_target="tpu_custom_call" | custom-call | flops 16000000000 | bytes 6291456 | tf_op jit(solution)/shard_map/attend/pallas_call | solution.py:445
  101.5 3.7 %collective-permute-done.27.refs_15_ = bf16[4,96,512]{2,1,0:T(8,128)(2,1)} collective-permute-done((bf16[4,96,512]{2,1,0:T(8,128)(2,1)}, bf16[4,96,512]{2,1,0:T(8,128)(2,1)}, u32[]{:S(2)}, u32[]{:S(2)}) %collective-permute-start.27) | collective-permute-done | bytes 393248 | tf_op jit(solution)/shard_map/ppermute | solution.py:78
  105.2 45.9 %feed_forward.1 = (f32[1024,768]{1,0:T(8,128)}, bf16[1024,3072]{1,0:T(8,128)(2,1)}, f32[4,1,768]{2,1,0:T(1,128)}, f32[1024,768]{1,0:T(8,128)}, bf16[1024,768]{1,...) custom-call(s32[4]{0:T(128)} %pad_add_fusion.place_ref, ...), custom_call_target="tpu_custom_call" | custom-call | flops 40000000000 | bytes 40000000 | tf_op jit(solution)/shard_map/feed_forward/pallas_call | solution.py:750
  151.7 11.8 %hidden_rows.1 = bf16[1024,768]{1,0:T(8,128)(2,1)} custom-call(s32[4]{0:T(128)} %pad_add_fusion.place_ref, bf16[1024,3072]{1,0:T(8,128)(2,1)} %get-tuple-element.197.act_ref, f32[1024,768]{1,0:T(8,128)} %get-tuple-element.198.resid_ref, f32[8,768]{1,0:T(8,128)} %stack.43.vec_ref, bf16[4,96,1024]{2,1,0:T(8,128)(2,1)} %constant_dynamic-update-slice_fusion.3.refs_0_, ...), custom_call_target="tpu_custom_call" | custom-call | flops 5000000000 | bytes 12000000 | tf_op jit(solution)/shard_map/hidden_rows/pallas_call | solution.py:835
  163.4 4.0 %sums.5 = (bf16[8,96,896]{2,1,0:T(8,128)(2,1)}, bf16[8,96,768]{2,1,0:T(8,128)(2,1)}) custom-call(bf16[16,96,896]{2,1,0:T(8,128)(2,1)} %get-tuple-element.200.refs_0_, bf16[16,96,896]{2,1,0:T(8,128)(2,1)} %collective-permute-done.28.refs_1_, bf16[16,96,768]{2,1,0:T(8,128)(2,1)} %get-tuple-element.202.refs_2_.refs_4_.refs_3_.refs_6_, ...), custom_call_target="tpu_custom_call" | custom-call | flops 1000000 | bytes 8000000 | tf_op jit(solution)/shard_map/sums/pallas_call | solution.py:145
  169.6 24.6 %attend_back.2 = (bf16[1024,512]{1,0:T(8,128)(2,1)}, bf16[1024,512]{1,0:T(8,128)(2,1)}, bf16[1024,512]{1,0:T(8,128)(2,1)}, bf16[16,96,640]{2,1,0:T(8,128)(2,1)}, bf16[16,96,640]{2,1,0:T(8,128)(2,1)}) custom-call(s32[1]{0:T(128)} %dynamic_slice.6.len_ref, s32[4]{0:T(128)} %pad_add_fusion.place_ref, bf16[1024,768]{1,0:T(8,128)(2,1)} %get-tuple-element.176.q_ref, ...), custom_call_target="tpu_custom_call" | custom-call | flops 12000000000 | bytes 20000000 | tf_op jit(solution)/shard_map/attend_back/pallas_call | solution.py:577
  197.0 15.3 %attend_back.3 = (bf16[1024,256]{1,0:T(8,128)(2,1)}, bf16[1024,256]{1,0:T(8,128)(2,1)}, bf16[1024,256]{1,0:T(8,128)(2,1)}, bf16[16,96,640]{2,1,0:T(8,128)(2,1)}, bf16[16,96,640]{2,1,0:T(8,128)(2,1)}) custom-call(s32[1]{0:T(128)} %dynamic_slice.6.len_ref, s32[4]{0:T(128)} %pad_add_fusion.place_ref, ...), custom_call_target="tpu_custom_call", output_to_operand_aliasing={{3}: (10, {}), {4}: (11, {})} | custom-call | flops 6000000000 | bytes 10000000 | tf_op jit(solution)/shard_map/attend_back/pallas_call | solution.py:577
  212.4 2.9 %sums.7 = (bf16[2,96,896]{2,1,0:T(8,128)(2,1)}, bf16[4,96,768]{2,1,0:T(8,128)(2,1)}) custom-call(bf16[16,96,896]{2,1,0:T(8,128)(2,1)} %get-tuple-element.200.refs_0_, bf16[16,96,896]{2,1,0:T(8,128)(2,1)} %collective-permute-done.28.refs_1_, bf16[8,96,896]{2,1,0:T(8,128)(2,1)} %collective-permute-done.30.refs_2_, ...), custom_call_target="tpu_custom_call" | custom-call | flops 1000000 | bytes 8000000 | tf_op jit(solution)/shard_map/sums/pallas_call | solution.py:145
  221.7 10.1 %input_grad.1 = (f32[1024,768]{1,0:T(8,128)}, f32[8,768]{1,0:T(8,128)}) custom-call(bf16[1024,512]{1,0:T(8,128)(2,1)} %get-tuple-element.233.refs_0_, bf16[1024,512]{1,0:T(8,128)(2,1)} %get-tuple-element.234.refs_1_, bf16[1024,512]{1,0:T(8,128)(2,1)} %get-tuple-element.235.refs_2_, bf16[1024,256]{1,0:T(8,128)(2,1)} %get-tuple-element.236.refs_3_, ...), custom_call_target="tpu_custom_call" | custom-call | flops 3623878656 | bytes 12582912 | tf_op jit(solution)/shard_map/input_grad/pallas_call | solution.py:884
  231.7 5.6 %collective-permute-done.35.refs_6_.refs_9_ = bf16[4,96,768]{2,1,0:T(8,128)(2,1)} collective-permute-done((bf16[4,96,768]{2,1,0:T(8,128)(2,1)}, bf16[4,96,768]{2,1,0:T(8,128)(2,1)}, u32[]{:S(2)}, u32[]{:S(2)}) %collective-permute-start.35) | collective-permute-done | bytes 589856 | tf_op jit(solution)/shard_map/ppermute | solution.py:78
  237.3 2.6 collective-permute-done.34.refs_2_.refs_14_
  240.7 2.7 sums.9
  246.0 3.6 %collective-permute-done.37 = f32[12,768]{1,0:T(8,128)S(1)} collective-permute-done((f32[12,768]{1,0:T(8,128)S(1)}, f32[12,768]{1,0:T(8,128)S(1)}, u32[]{:S(2)}, u32[]{:S(2)}) %collective-permute-start.37) | collective-permute-done | bytes 36896 | tf_op jit(solution)/shard_map/ppermute | solution.py:78
  253.7 6.7 %collective-permute-done.40.refs_10_ = bf16[2,96,768]{2,1,0:T(8,128)(2,1)S(1)} collective-permute-done((bf16[2,96,768]{2,1,0:T(8,128)(2,1)}, bf16[2,96,768]{2,1,0:T(8,128)(2,1)S(1)}, u32[]{:S(2)}, u32[]{:S(2)}) %collective-permute-start.40) | collective-permute-done | bytes 294944 | tf_op jit(solution)/shard_map/ppermute | solution.py:78
  266.4 10.1 %collective-permute-done.43 = f32[12,768]{1,0:T(8,128)S(1)} collective-permute-done((f32[12,768]{1,0:T(8,128)S(1)}, f32[12,768]{1,0:T(8,128)S(1)}, u32[]{:S(2)}, u32[]{:S(2)}) %collective-permute-start.43) | collective-permute-done | bytes 36896 | tf_op jit(solution)/shard_map/ppermute | solution.py:78
  284.5 2.8 last_sums.1
  (200 shorter events, 70.7 us)
Async XLA Ops:
  13.2 15.1 %collective-permute-start.4 = (bf16[1,96,1024]{2,1,0:T(8,128)(2,1)S(1)}, bf16[1,96,1024]{2,1,0:T(8,128)(2,1)S(1)}, u32[]{:S(2)}, u32[]{:S(2)}) collective-permute-start(bf16[1,96,1024]{2,1,0:T(8,128)(2,1)S(1)} %pad_maximum_fusion.2), channel_id=1, source_target_pairs={{0,8},{1,9},{2,10},{3,11},{4,12},{5,13},{6,14},{7,15},{8,24},{9,25... | collective-permute-start | bytes 589832 | tf_op jit(solution)/shard_map/ppermute | solution.py:78
  14.8 17.4 %collective-permute-start.1 = (bf16[2,96,768]{2,1,0:T(8,128)(2,1)S(1)}, bf16[2,96,768]{2,1,0:T(8,128)(2,1)S(1)}, u32[]{:S(2)}, u32[]{:S(2)}) collective-permute-start(bf16[2,96,768]{2,1,0:T(8,128)(2,1)S(1)} %pad_maximum_fusion.1), channel_id=1, source_target_pairs={{0,16},{1,17},{2,18},{3,19},{4,20},{5,21},{6,22},{7,23},{8,24},{9,... | collective-permute-start | bytes 884744 | tf_op jit(solution)/shard_map/ppermute | solution.py:78
  32.3 17.9 %collective-permute-start.6 = (bf16[4,96,768]{2,1,0:T(8,128)(2,1)S(1)}, bf16[4,96,768]{2,1,0:T(8,128)(2,1)S(1)}, u32[]{:S(2)}, u32[]{:S(2)}) collective-permute-start(bf16[4,96,768]{2,1,0:T(8,128)(2,1)S(1)} %pad_maximum_fusion.refs_0_), channel_id=1, source_target_pairs={{0,2},{1,5},{2,0},{3,7},{4,6},{5,1},{6,4},{7,3},{8,10},{9,13},{10,... | collective-permute-start | bytes 1769480 | tf_op jit(solution)/shard_map/ppermute | solution.py:78
  33.0 17.2 %collective-permute-start.5 = (bf16[4,96,768]{2,1,0:T(8,128)(2,1)S(1)}, bf16[4,96,768]{2,1,0:T(8,128)(2,1)S(1)}, u32[]{:S(2)}, u32[]{:S(2)}) collective-permute-start(bf16[4,96,768]{2,1,0:T(8,128)(2,1)S(1)} %pad_maximum_fusion.refs_0_), channel_id=1, source_target_pairs={{0,4},{1,3},{2,6},{3,1},{4,0},{5,7},{6,2},{7,5},{8,12},{9,11},{10,... | collective-permute-start | bytes 1769480 | tf_op jit(solution)/shard_map/ppermute | solution.py:78
  35.7 14.5 %collective-permute-start.8 = (bf16[4,96,512]{2,1,0:T(8,128)(2,1)}, bf16[4,96,512]{2,1,0:T(8,128)(2,1)}, u32[]{:S(2)}, u32[]{:S(2)}) collective-permute-start(bf16[4,96,512]{2,1,0:T(8,128)(2,1)} %constant_dynamic-update-slice_fusion.refs_8_), channel_id=1, source_target_pairs={{0,8},{1,9},{2,10},{3,11},{4,12},{5,13},{6,14},{7,15},{8,24},{9,25... | collective-permute-start | bytes 1179656 | tf_op jit(solution)/shard_map/ppermute | solution.py:78
  39.9 14.7 %collective-permute-start.11 = (bf16[4,96,768]{2,1,0:T(8,128)(2,1)S(1)}, bf16[4,96,768]{2,1,0:T(8,128)(2,1)S(1)}, u32[]{:S(2)}, u32[]{:S(2)}) collective-permute-start(bf16[4,96,768]{2,1,0:T(8,128)(2,1)S(1)} %pad_maximum_fusion.refs_0_), channel_id=1, source_target_pairs={{0,1},{1,0},{2,3},{3,2},{4,5},{5,4},{6,7},{7,6},{8,9},{9,8},{10,11... | collective-permute-start | bytes 1769480 | tf_op jit(solution)/shard_map/ppermute | solution.py:78
  62.1 16.5 %collective-permute-start.14 = (bf16[4,96,1024]{2,1,0:T(8,128)(2,1)}, bf16[4,96,1024]{2,1,0:T(8,128)(2,1)}, u32[]{:S(2)}, u32[]{:S(2)}) collective-permute-start(bf16[4,96,1024]{2,1,0:T(8,128)(2,1)} %constant_dynamic-update-slice_fusion.3.refs_0_), channel_id=1, source_target_pairs={{0,4},{1,3},{2,6},{3,1},{4,0},{5,7},{6,2},{7,5},{8,12},{9,11},{10,... | collective-permute-start | bytes 2359304 | tf_op jit(solution)/shard_map/ppermute | solution.py:78
  62.5 19.7 %collective-permute-start.20 = (bf16[4,96,1024]{2,1,0:T(8,128)(2,1)}, bf16[4,96,1024]{2,1,0:T(8,128)(2,1)}, u32[]{:S(2)}, u32[]{:S(2)}) collective-permute-start(bf16[4,96,1024]{2,1,0:T(8,128)(2,1)} %constant_dynamic-update-slice_fusion.3.refs_0_), channel_id=1, source_target_pairs={{0,1},{1,0},{2,3},{3,2},{4,5},{5,4},{6,7},{7,6},{8,9},{9,8},{10,11... | collective-permute-start | bytes 2359304 | tf_op jit(solution)/shard_map/ppermute | solution.py:78
  65.5 16.7 %collective-permute-start.23 = (bf16[4,96,512]{2,1,0:T(8,128)(2,1)}, bf16[4,96,512]{2,1,0:T(8,128)(2,1)}, u32[]{:S(2)}, u32[]{:S(2)}) collective-permute-start(bf16[4,96,512]{2,1,0:T(8,128)(2,1)} %collective-permute-done.8.refs_9_), channel_id=1, source_target_pairs={{0,1},{1,0},{2,3},{3,2},{4,5},{5,4},{6,7},{7,6},{8,9},{9,8},{10,11... | collective-permute-start | bytes 1179656 | tf_op jit(solution)/shard_map/ppermute | solution.py:78
  78.1 22.6 %collective-permute-start.17 = (bf16[4,96,1024]{2,1,0:T(8,128)(2,1)}, bf16[4,96,1024]{2,1,0:T(8,128)(2,1)}, u32[]{:S(2)}, u32[]{:S(2)}) collective-permute-start(bf16[4,96,1024]{2,1,0:T(8,128)(2,1)} %constant_dynamic-update-slice_fusion.3.refs_0_), channel_id=1, source_target_pairs={{0,2},{1,5},{2,0},{3,7},{4,6},{5,1},{6,4},{7,3},{8,10},{9,13},{10,... | collective-permute-start | bytes 2359304 | tf_op jit(solution)/shard_map/ppermute | solution.py:78
  78.6 22.2 %collective-permute-start.24 = (bf16[4,96,512]{2,1,0:T(8,128)(2,1)}, bf16[4,96,512]{2,1,0:T(8,128)(2,1)}, u32[]{:S(2)}, u32[]{:S(2)}) collective-permute-start(bf16[4,96,512]{2,1,0:T(8,128)(2,1)} %collective-permute-done.15.refs_10_), channel_id=1, source_target_pairs={{0,1},{1,0},{2,3},{3,2},{4,5},{5,4},{6,7},{7,6},{8,9},{9,8},{10,11... | collective-permute-start | bytes 1179656 | tf_op jit(solution)/shard_map/ppermute | solution.py:78
  78.6 22.2 %collective-permute-start.19 = (bf16[4,96,512]{2,1,0:T(8,128)(2,1)}, bf16[4,96,512]{2,1,0:T(8,128)(2,1)}, u32[]{:S(2)}, u32[]{:S(2)}) collective-permute-start(bf16[4,96,512]{2,1,0:T(8,128)(2,1)} %collective-permute-done.15.refs_10_), channel_id=1, source_target_pairs={{0,8},{1,9},{2,10},{3,11},{4,12},{5,13},{6,14},{7,15},{8,24},{9,25... | collective-permute-start | bytes 1179656 | tf_op jit(solution)/shard_map/ppermute | solution.py:78
  82.2 18.6 %collective-permute-start.21 = (bf16[4,96,1024]{2,1,0:T(8,128)(2,1)}, bf16[4,96,1024]{2,1,0:T(8,128)(2,1)}, u32[]{:S(2)}, u32[]{:S(2)}) collective-permute-start(bf16[4,96,1024]{2,1,0:T(8,128)(2,1)} %collective-permute-done.14.refs_1_), channel_id=1, source_target_pairs={{0,1},{1,0},{2,3},{3,2},{4,5},{5,4},{6,7},{7,6},{8,9},{9,8},{10,11... | collective-permute-start | bytes 2359304 | tf_op jit(solution)/shard_map/ppermute | solution.py:78
  82.2 18.6 %collective-permute-start.18 = (bf16[4,96,1024]{2,1,0:T(8,128)(2,1)}, bf16[4,96,1024]{2,1,0:T(8,128)(2,1)}, u32[]{:S(2)}, u32[]{:S(2)}) collective-permute-start(bf16[4,96,1024]{2,1,0:T(8,128)(2,1)} %collective-permute-done.14.refs_1_), channel_id=1, source_target_pairs={{0,2},{1,5},{2,0},{3,7},{4,6},{5,1},{6,4},{7,3},{8,10},{9,13},{10,... | collective-permute-start | bytes 2359304 | tf_op jit(solution)/shard_map/ppermute | solution.py:78
  167.5 26.7 %collective-permute-start.30 = (bf16[8,96,896]{2,1,0:T(8,128)(2,1)}, bf16[8,96,896]{2,1,0:T(8,128)(2,1)}, u32[]{:S(2)}, u32[]{:S(2)}) collective-permute-start(bf16[8,96,896]{2,1,0:T(8,128)(2,1)} %get-tuple-element.204), channel_id=1, source_target_pairs={{0,2},{1,5},{2,0},{3,7},{4,6},{5,1},{6,4},{7,3},{8,10},{9,13},{10,... | collective-permute-start | bytes 4128776 | tf_op jit(solution)/shard_map/ppermute | solution.py:78
  167.9 44.4 %collective-permute-start.32 = (bf16[8,96,768]{2,1,0:T(8,128)(2,1)}, bf16[8,96,768]{2,1,0:T(8,128)(2,1)}, u32[]{:S(2)}, u32[]{:S(2)}) collective-permute-start(bf16[8,96,768]{2,1,0:T(8,128)(2,1)} %get-tuple-element.216), channel_id=1, source_target_pairs={{0,2},{1,5},{2,0},{3,7},{4,6},{5,1},{6,4},{7,3},{8,10},{9,13},{10,... | collective-permute-start | bytes 3538952 | tf_op jit(solution)/shard_map/ppermute | solution.py:78
  196.6 15.8 %collective-permute-start.31 = (bf16[4,96,896]{2,1,0:T(8,128)(2,1)}, bf16[4,96,896]{2,1,0:T(8,128)(2,1)}, u32[]{:S(2)}, u32[]{:S(2)}) collective-permute-start(bf16[4,96,896]{2,1,0:T(8,128)(2,1)} %sums.6), channel_id=1, source_target_pairs={{0,4},{1,3},{2,6},{3,1},{4,0},{5,7},{6,2},{7,5},{8,12},{9,11},{10,... | collective-permute-start | bytes 2064392 | tf_op jit(solution)/shard_map/ppermute | solution.py:78
  219.1 20.8 %collective-permute-start.34 = (bf16[8,96,640]{2,1,0:T(8,128)(2,1)}, bf16[8,96,640]{2,1,0:T(8,128)(2,1)}, u32[]{:S(2)}, u32[]{:S(2)}) collective-permute-start(bf16[8,96,640]{2,1,0:T(8,128)(2,1)} %sums.8), channel_id=1, source_target_pairs={{0,2},{1,5},{2,0},{3,7},{4,6},{5,1},{6,4},{7,3},{8,10},{9,13},{10,... | collective-permute-start | bytes 2949128 | tf_op jit(solution)/shard_map/ppermute | solution.py:78
  220.7 16.6 %collective-permute-start.35 = (bf16[4,96,768]{2,1,0:T(8,128)(2,1)}, bf16[4,96,768]{2,1,0:T(8,128)(2,1)}, u32[]{:S(2)}, u32[]{:S(2)}) collective-permute-start(bf16[4,96,768]{2,1,0:T(8,128)(2,1)} %get-tuple-element.232), channel_id=1, source_target_pairs={{0,4},{1,3},{2,6},{3,1},{4,0},{5,7},{6,2},{7,5},{8,12},{9,11},{10,... | collective-permute-start | bytes 1769480 | tf_op jit(solution)/shard_map/ppermute | solution.py:78
  221.2 22.2 %collective-permute-start.38 = (bf16[2,96,896]{2,1,0:T(8,128)(2,1)}, bf16[2,96,896]{2,1,0:T(8,128)(2,1)}, u32[]{:S(2)}, u32[]{:S(2)}) collective-permute-start(bf16[2,96,896]{2,1,0:T(8,128)(2,1)} %get-tuple-element.247), channel_id=1, source_target_pairs={{0,16},{1,17},{2,18},{3,19},{4,20},{5,21},{6,22},{7,23},{8,24},{9,... | collective-permute-start | bytes 1032200 | tf_op jit(solution)/shard_map/ppermute | solution.py:78
  243.4 17.0 %collective-permute-start.40 = (bf16[2,96,768]{2,1,0:T(8,128)(2,1)}, bf16[2,96,768]{2,1,0:T(8,128)(2,1)S(1)}, u32[]{:S(2)}, u32[]{:S(2)}) collective-permute-start(bf16[2,96,768]{2,1,0:T(8,128)(2,1)} %get-tuple-element.253), channel_id=1, source_target_pairs={{0,16},{1,17},{2,18},{3,19},{4,20},{5,21},{6,22},{7,23},{8,24},{9,... | collective-permute-start | bytes 884744 | tf_op jit(solution)/shard_map/ppermute | solution.py:78
  243.9 16.5 %collective-permute-start.39 = (bf16[4,96,640]{2,1,0:T(8,128)(2,1)}, bf16[4,96,640]{2,1,0:T(8,128)(2,1)S(1)}, u32[]{:S(2)}, u32[]{:S(2)}) collective-permute-start(bf16[4,96,640]{2,1,0:T(8,128)(2,1)} %get-tuple-element.252), channel_id=1, source_target_pairs={{0,4},{1,3},{2,6},{3,1},{4,0},{5,7},{6,2},{7,5},{8,12},{9,11},{10,... | collective-permute-start | bytes 1474568 | tf_op jit(solution)/shard_map/ppermute | solution.py:78
  252.1 14.3 %collective-permute-start.44 = (bf16[1,96,896]{2,1,0:T(8,128)(2,1)S(1)}, bf16[1,96,896]{2,1,0:T(8,128)(2,1)S(1)}, u32[]{:S(2)}, u32[]{:S(2)}) collective-permute-start(bf16[1,96,896]{2,1,0:T(8,128)(2,1)S(1)} %add_convert_fusion.1), channel_id=1, source_target_pairs={{0,8},{1,9},{2,10},{3,11},{4,12},{5,13},{6,14},{7,15},{8,0},{9,1},... | collective-permute-start | bytes 516104 | tf_op jit(solution)/shard_map/ppermute | solution.py:78
  262.0 14.5 %collective-permute-start.42 = (bf16[2,96,640]{2,1,0:T(8,128)(2,1)S(1)}, bf16[2,96,640]{2,1,0:T(8,128)(2,1)S(1)}, u32[]{:S(2)}, u32[]{:S(2)}) collective-permute-start(bf16[2,96,640]{2,1,0:T(8,128)(2,1)S(1)} %add_convert_fusion), channel_id=1, source_target_pairs={{0,16},{1,17},{2,18},{3,19},{4,20},{5,21},{6,22},{7,23},{8,24},{9,... | collective-permute-start | bytes 737288 | tf_op jit(solution)/shard_map/ppermute | solution.py:78
  (50 other events, 436.9 us)

commit v2 on v1

--- a/solution.py
+++ b/solution.py
@@ -1088,16 +1088,14 @@
         came_small = exchange(small, flip_second)
         small = small + came_small
         came_small = exchange(small, flip_first)
-        came_rest, came_down, came_small = after(came_rest, came_down, came_small)
+        came_rest, came_small = after(came_rest, came_small)
         (rest.sent,) = plain_sums(rest.want(came_rest))
         small = small + came_small
-        rest.sent, came_down = after(rest.sent, came_down)
         came_rest, came_small = rest.step(), exchange(small, flip_far)
+        came_small, came_down = after(came_small, came_down)
         (down.sent,) = plain_sums(down.want(came_down))
         came_down = down.step()
-        came_rest, came_small, came_up, came_down = after(
-            came_rest, came_small, came_up, came_down
-        )
+        came_rest, came_small, came_up = after(came_rest, came_small, came_up)
         (rest.sent,) = plain_sums(rest.want(came_rest))
         small = small + came_small
         came_rest, came_small = rest.step(), exchange(small, flip_near)

time: 289 us -> 287 us (level)
  transfers between devices with their start and end apart: 48 -> 48, of which waited for: 16 -> 16; matrix products, arithmetic and copies ran while one was open for 7% -> 7% of each run, Pallas kernels for 34% -> 35%
where the time goes in v2:
time: 287 us; the launch traced here: 286 us
  Pallas kernels  154 us (54%)
  waiting for transfers between devices  61.4 us (21%)
  starting transfers between devices  44.2 us (15%)
  local copies, waits for them, and re-layouts  13.8 us (5%)
  other arithmetic  11.2 us (4%)
    ppermute x48, waiting for transfers between devices, exchange(): return lax.ppermute(array, BOTH, pairs)  61.4 us
    pallas_call x1, Pallas kernels, feed_forward(): pl.pallas_call(functools.partial(feed_kernel, counts), grid_spec=pltpu.Pr...  45.9 us
    ppermute x48, starting transfers between devices, exchange(): return lax.ppermute(array, BOTH, pairs)  44.2 us
    pallas_call x2, Pallas kernels, attend_back(): pl.pallas_call(functools.partial(attend_back_kernel, first, len(grads), b...  39.9 us
    pallas_call x1, Pallas kernels, attend(): pl.pallas_call(attend_kernel, grid_spec=pltpu.PrefetchScalarGridSpec(num_...  16.8 us
    pallas_call x5, Pallas kernels, sums(): pl.pallas_call(functools.partial(sums_kernel, plan), in_specs=[ANY_SPEC]...  14.4 us
    pallas_call x1, Pallas kernels, project(): pl.pallas_call(functools.partial(qkv_kernel, len(sources)), grid_spec=plt...  12.1 us
    pallas_call x1, Pallas kernels, hidden_rows(): pl.pallas_call(functools.partial(hidden_kernel, counts), grid_spec=pltpu....  11.8 us
  transfers between devices with their start and end apart: 48, of which 16 were waited for; matrix products, arithmetic and copies ran while one was open for 7% of the time, Pallas kernels for 35%

profile of v2, /device:TPU:0, one launch (start us, length us, event | category | flops | bytes accessed | tf_op | source)
XLA Modules:
  0.0 285.9 jit_solution(7170595504851446305)
XLA Ops:
  3.1 3.1 %collective-permute-start = (bf16[1,96,768]{2,1,0:T(8,128)(2,1)S(1)}, bf16[1,96,768]{2,1,0:T(8,128)(2,1)S(1)}, u32[]{:S(2)}, u32[]{:S(2)}) collective-permute-start(bf16[1,96,768]{2,1,0:T(8,128)(2,1)S(1)} %bitcast.37), channel_id=1, source_target_pairs={{0,8},{1,9},{2,10},{3,11},{4,12},{5,13},{6,14},{7,15},{8,0},{9,1},... | collective-permute-start | bytes 442376 | tf_op jit(solution)/shard_map/ppermute | solution.py:78
  23.1 5.1 %collective-permute-done.4 = bf16[1,96,1024]{2,1,0:T(8,128)(2,1)S(1)} collective-permute-done((bf16[1,96,1024]{2,1,0:T(8,128)(2,1)S(1)}, bf16[1,96,1024]{2,1,0:T(8,128)(2,1)S(1)}, u32[]{:S(2)}, u32[]{:S(2)}) %collective-permute-start.4) | collective-permute-done | bytes 196640 | tf_op jit(solution)/shard_map/ppermute | solution.py:78
  28.2 4.0 %collective-permute-done.1 = bf16[2,96,768]{2,1,0:T(8,128)(2,1)S(1)} collective-permute-done((bf16[2,96,768]{2,1,0:T(8,128)(2,1)S(1)}, bf16[2,96,768]{2,1,0:T(8,128)(2,1)S(1)}, u32[]{:S(2)}, u32[]{:S(2)}) %collective-permute-start.1) | collective-permute-done | bytes 294944 | tf_op jit(solution)/shard_map/ppermute | solution.py:78
  36.5 3.4 %collective-permute-start.7 = (bf16[1,96,1024]{2,1,0:T(8,128)(2,1)S(1)}, bf16[1,96,1024]{2,1,0:T(8,128)(2,1)S(1)}, u32[]{:S(2)}, u32[]{:S(2)}) collective-permute-start(bf16[1,96,1024]{2,1,0:T(8,128)(2,1)S(1)} %collective-permute-done.4), channel_id=1, source_target_pairs={{0,8},{1,9},{2,10},{3,11},{4,12},{5,13},{6,14},{7,15},{8,24},{9,25... | collective-permute-start | bytes 589832 | tf_op jit(solution)/shard_map/ppermute | solution.py:78
  39.9 10.3 %collective-permute-done.7 = bf16[1,96,1024]{2,1,0:T(8,128)(2,1)S(1)} collective-permute-done((bf16[1,96,1024]{2,1,0:T(8,128)(2,1)S(1)}, bf16[1,96,1024]{2,1,0:T(8,128)(2,1)S(1)}, u32[]{:S(2)}, u32[]{:S(2)}) %collective-permute-start.7) | collective-permute-done | bytes 196640 | tf_op jit(solution)/shard_map/ppermute | solution.py:78
  54.6 4.6 %collective-permute-done.10 = bf16[1,96,1024]{2,1,0:T(8,128)(2,1)S(1)} collective-permute-done((bf16[1,96,1024]{2,1,0:T(8,128)(2,1)S(1)}, bf16[1,96,1024]{2,1,0:T(8,128)(2,1)S(1)}, u32[]{:S(2)}, u32[]{:S(2)}) %collective-permute-start.10) | collective-permute-done | bytes 196640 | tf_op jit(solution)/shard_map/ppermute | solution.py:78
  66.0 12.1 %project.1 = (bf16[1024,768]{1,0:T(8,128)(2,1)}, bf16[1024,768]{1,0:T(8,128)(2,1)}, bf16[1024,768]{1,0:T(8,128)(2,1)}, bf16[1024,768]{1,0:T(8,128)(2,1)}, bf16[4,768,768]{2,1,0:T(8,128)(2,1)}) custom-call(s32[4]{0:T(128)} %pad_add_fusion.place_ref, bf16[1024,768]{1,0:T(8,128)(2,1)} %refs_7_.1, f32[1,768]{1,0:T(1,128)} %broadcast_in_dim.13.gain_ref.refs_9_, ...), custom_call_target="tpu_custom_call" | custom-call | flops 3623878656 | bytes 12582912 | tf_op jit(solution)/shard_map/project/pallas_call | solution.py:362
  78.6 3.6 %collective-permute-start.19 = (bf16[4,96,512]{2,1,0:T(8,128)(2,1)}, bf16[4,96,512]{2,1,0:T(8,128)(2,1)}, u32[]{:S(2)}, u32[]{:S(2)}) collective-permute-start(bf16[4,96,512]{2,1,0:T(8,128)(2,1)} %collective-permute-done.15.refs_10_), channel_id=1, source_target_pairs={{0,8},{1,9},{2,10},{3,11},{4,12},{5,13},{6,14},{7,15},{8,24},{9,25... | collective-permute-start | bytes 1179656 | tf_op jit(solution)/shard_map/ppermute | solution.py:78
  84.0 16.8 %attend.1 = (bf16[1024,768]{1,0:T(8,128)(2,1)}, f32[6,8,1024]{2,1,0:T(8,128)}) custom-call(s32[1]{0:T(128)} %dynamic_slice.6.len_ref, bf16[1024,768]{1,0:T(8,128)(2,1)} %get-tuple-element.174.q_ref, bf16[1024,768]{1,0:T(8,128)(2,1)} %get-tuple-element.175.k_ref, bf16[1024,768]{1,0:T(8,128)(2,1)} %get-tuple-element.176.v_ref), custom_call_target="tpu_custom_call" | custom-call | flops 16000000000 | bytes 6291456 | tf_op jit(solution)/shard_map/attend/pallas_call | solution.py:445
  101.5 3.7 %collective-permute-done.27.refs_15_ = bf16[4,96,512]{2,1,0:T(8,128)(2,1)} collective-permute-done((bf16[4,96,512]{2,1,0:T(8,128)(2,1)}, bf16[4,96,512]{2,1,0:T(8,128)(2,1)}, u32[]{:S(2)}, u32[]{:S(2)}) %collective-permute-start.27) | collective-permute-done | bytes 393248 | tf_op jit(solution)/shard_map/ppermute | solution.py:78
  105.2 45.9 %feed_forward.1 = (f32[1024,768]{1,0:T(8,128)}, bf16[1024,3072]{1,0:T(8,128)(2,1)}, f32[4,1,768]{2,1,0:T(1,128)}, f32[1024,768]{1,0:T(8,128)}, bf16[1024,768]{1,...) custom-call(s32[4]{0:T(128)} %pad_add_fusion.place_ref, ...), custom_call_target="tpu_custom_call" | custom-call | flops 40000000000 | bytes 40000000 | tf_op jit(solution)/shard_map/feed_forward/pallas_call | solution.py:750
  151.7 11.8 %hidden_rows.1 = bf16[1024,768]{1,0:T(8,128)(2,1)} custom-call(s32[4]{0:T(128)} %pad_add_fusion.place_ref, bf16[1024,3072]{1,0:T(8,128)(2,1)} %get-tuple-element.195.act_ref, f32[1024,768]{1,0:T(8,128)} %get-tuple-element.196.resid_ref, f32[8,768]{1,0:T(8,128)} %stack.43.vec_ref, bf16[4,96,1024]{2,1,0:T(8,128)(2,1)} %constant_dynamic-update-slice_fusion.3.refs_0_, ...), custom_call_target="tpu_custom_call" | custom-call | flops 5000000000 | bytes 12000000 | tf_op jit(solution)/shard_map/hidden_rows/pallas_call | solution.py:835
  163.4 4.0 %sums.5 = (bf16[8,96,896]{2,1,0:T(8,128)(2,1)}, bf16[8,96,768]{2,1,0:T(8,128)(2,1)}) custom-call(bf16[16,96,896]{2,1,0:T(8,128)(2,1)} %get-tuple-element.198.refs_0_, bf16[16,96,896]{2,1,0:T(8,128)(2,1)} %collective-permute-done.28.refs_1_, bf16[16,96,768]{2,1,0:T(8,128)(2,1)} %get-tuple-element.200.refs_2_.refs_4_.refs_3_.refs_6_, ...), custom_call_target="tpu_custom_call" | custom-call | flops 1000000 | bytes 8000000 | tf_op jit(solution)/shard_map/sums/pallas_call | solution.py:145
  169.6 24.6 %attend_back.2 = (bf16[1024,512]{1,0:T(8,128)(2,1)}, bf16[1024,512]{1,0:T(8,128)(2,1)}, bf16[1024,512]{1,0:T(8,128)(2,1)}, bf16[16,96,640]{2,1,0:T(8,128)(2,1)}, bf16[16,96,640]{2,1,0:T(8,128)(2,1)}) custom-call(s32[1]{0:T(128)} %dynamic_slice.6.len_ref, s32[4]{0:T(128)} %pad_add_fusion.place_ref, bf16[1024,768]{1,0:T(8,128)(2,1)} %get-tuple-element.174.q_ref, ...), custom_call_target="tpu_custom_call" | custom-call | flops 12000000000 | bytes 20000000 | tf_op jit(solution)/shard_map/attend_back/pallas_call | solution.py:577
  197.0 15.3 %attend_back.3 = (bf16[1024,256]{1,0:T(8,128)(2,1)}, bf16[1024,256]{1,0:T(8,128)(2,1)}, bf16[1024,256]{1,0:T(8,128)(2,1)}, bf16[16,96,640]{2,1,0:T(8,128)(2,1)}, bf16[16,96,640]{2,1,0:T(8,128)(2,1)}) custom-call(s32[1]{0:T(128)} %dynamic_slice.6.len_ref, s32[4]{0:T(128)} %pad_add_fusion.place_ref, ...), custom_call_target="tpu_custom_call", output_to_operand_aliasing={{3}: (10, {}), {4}: (11, {})} | custom-call | flops 6000000000 | bytes 10000000 | tf_op jit(solution)/shard_map/attend_back/pallas_call | solution.py:577
  212.4 2.9 %sums.7 = (bf16[2,96,896]{2,1,0:T(8,128)(2,1)}, bf16[4,96,768]{2,1,0:T(8,128)(2,1)}) custom-call(bf16[16,96,896]{2,1,0:T(8,128)(2,1)} %get-tuple-element.198.refs_0_, bf16[16,96,896]{2,1,0:T(8,128)(2,1)} %collective-permute-done.28.refs_1_, bf16[8,96,896]{2,1,0:T(8,128)(2,1)} %collective-permute-done.30.refs_2_, ...), custom_call_target="tpu_custom_call" | custom-call | flops 1000000 | bytes 8000000 | tf_op jit(solution)/shard_map/sums/pallas_call | solution.py:145
  221.7 10.1 %input_grad.1 = (f32[1024,768]{1,0:T(8,128)}, f32[8,768]{1,0:T(8,128)}) custom-call(bf16[1024,512]{1,0:T(8,128)(2,1)} %get-tuple-element.231.refs_0_, bf16[1024,512]{1,0:T(8,128)(2,1)} %get-tuple-element.232.refs_1_, bf16[1024,512]{1,0:T(8,128)(2,1)} %get-tuple-element.233.refs_2_, bf16[1024,256]{1,0:T(8,128)(2,1)} %get-tuple-element.234.refs_3_, ...), custom_call_target="tpu_custom_call" | custom-call | flops 3623878656 | bytes 12582912 | tf_op jit(solution)/shard_map/input_grad/pallas_call | solution.py:884
  231.7 5.6 %collective-permute-done.35.refs_6_.refs_9_ = bf16[4,96,768]{2,1,0:T(8,128)(2,1)} collective-permute-done((bf16[4,96,768]{2,1,0:T(8,128)(2,1)}, bf16[4,96,768]{2,1,0:T(8,128)(2,1)}, u32[]{:S(2)}, u32[]{:S(2)}) %collective-permute-start.35) | collective-permute-done | bytes 589856 | tf_op jit(solution)/shard_map/ppermute | solution.py:78
  237.3 2.6 collective-permute-done.34.refs_2_.refs_14_
  240.7 2.7 sums.9
  246.0 3.2 %collective-permute-done.37 = f32[12,768]{1,0:T(8,128)S(1)} collective-permute-done((f32[12,768]{1,0:T(8,128)S(1)}, f32[12,768]{1,0:T(8,128)S(1)}, u32[]{:S(2)}, u32[]{:S(2)}) %collective-permute-start.37) | collective-permute-done | bytes 36896 | tf_op jit(solution)/shard_map/ppermute | solution.py:78
  257.9 11.3 %collective-permute-done.43.refs_10_ = bf16[2,96,768]{2,1,0:T(8,128)(2,1)S(1)} collective-permute-done((bf16[2,96,768]{2,1,0:T(8,128)(2,1)}, bf16[2,96,768]{2,1,0:T(8,128)(2,1)S(1)}, u32[]{:S(2)}, u32[]{:S(2)}) %collective-permute-start.43) | collective-permute-done | bytes 294944 | tf_op jit(solution)/shard_map/ppermute | solution.py:78
  271.6 3.1 %collective-permute-done.41.refs_16_ = bf16[2,96,640]{2,1,0:T(8,128)(2,1)S(1)} collective-permute-done((bf16[2,96,640]{2,1,0:T(8,128)(2,1)S(1)}, bf16[2,96,640]{2,1,0:T(8,128)(2,1)S(1)}, u32[]{:S(2)}, u32[]{:S(2)}) %collective-permute-start.41) | collective-permute-done | bytes 245792 | tf_op jit(solution)/shard_map/ppermute | solution.py:78
  282.9 2.8 last_sums.1
  (200 shorter events, 71.9 us)
Async XLA Ops:
  13.2 15.1 %collective-permute-start.4 = (bf16[1,96,1024]{2,1,0:T(8,128)(2,1)S(1)}, bf16[1,96,1024]{2,1,0:T(8,128)(2,1)S(1)}, u32[]{:S(2)}, u32[]{:S(2)}) collective-permute-start(bf16[1,96,1024]{2,1,0:T(8,128)(2,1)S(1)} %pad_maximum_fusion.2), channel_id=1, source_target_pairs={{0,8},{1,9},{2,10},{3,11},{4,12},{5,13},{6,14},{7,15},{8,24},{9,25... | collective-permute-start | bytes 589832 | tf_op jit(solution)/shard_map/ppermute | solution.py:78
  14.8 17.4 %collective-permute-start.1 = (bf16[2,96,768]{2,1,0:T(8,128)(2,1)S(1)}, bf16[2,96,768]{2,1,0:T(8,128)(2,1)S(1)}, u32[]{:S(2)}, u32[]{:S(2)}) collective-permute-start(bf16[2,96,768]{2,1,0:T(8,128)(2,1)S(1)} %pad_maximum_fusion.1), channel_id=1, source_target_pairs={{0,16},{1,17},{2,18},{3,19},{4,20},{5,21},{6,22},{7,23},{8,24},{9,... | collective-permute-start | bytes 884744 | tf_op jit(solution)/shard_map/ppermute | solution.py:78
  32.3 17.9 %collective-permute-start.6 = (bf16[4,96,768]{2,1,0:T(8,128)(2,1)S(1)}, bf16[4,96,768]{2,1,0:T(8,128)(2,1)S(1)}, u32[]{:S(2)}, u32[]{:S(2)}) collective-permute-start(bf16[4,96,768]{2,1,0:T(8,128)(2,1)S(1)} %pad_maximum_fusion.refs_0_), channel_id=1, source_target_pairs={{0,2},{1,5},{2,0},{3,7},{4,6},{5,1},{6,4},{7,3},{8,10},{9,13},{10,... | collective-permute-start | bytes 1769480 | tf_op jit(solution)/shard_map/ppermute | solution.py:78
  33.0 17.2 %collective-permute-start.5 = (bf16[4,96,768]{2,1,0:T(8,128)(2,1)S(1)}, bf16[4,96,768]{2,1,0:T(8,128)(2,1)S(1)}, u32[]{:S(2)}, u32[]{:S(2)}) collective-permute-start(bf16[4,96,768]{2,1,0:T(8,128)(2,1)S(1)} %pad_maximum_fusion.refs_0_), channel_id=1, source_target_pairs={{0,4},{1,3},{2,6},{3,1},{4,0},{5,7},{6,2},{7,5},{8,12},{9,11},{10,... | collective-permute-start | bytes 1769480 | tf_op jit(solution)/shard_map/ppermute | solution.py:78
  35.7 14.5 %collective-permute-start.8 = (bf16[4,96,512]{2,1,0:T(8,128)(2,1)}, bf16[4,96,512]{2,1,0:T(8,128)(2,1)}, u32[]{:S(2)}, u32[]{:S(2)}) collective-permute-start(bf16[4,96,512]{2,1,0:T(8,128)(2,1)} %constant_dynamic-update-slice_fusion.refs_8_), channel_id=1, source_target_pairs={{0,8},{1,9},{2,10},{3,11},{4,12},{5,13},{6,14},{7,15},{8,24},{9,25... | collective-permute-start | bytes 1179656 | tf_op jit(solution)/shard_map/ppermute | solution.py:78
  39.9 14.7 %collective-permute-start.11 = (bf16[4,96,768]{2,1,0:T(8,128)(2,1)S(1)}, bf16[4,96,768]{2,1,0:T(8,128)(2,1)S(1)}, u32[]{:S(2)}, u32[]{:S(2)}) collective-permute-start(bf16[4,96,768]{2,1,0:T(8,128)(2,1)S(1)} %pad_maximum_fusion.refs_0_), channel_id=1, source_target_pairs={{0,1},{1,0},{2,3},{3,2},{4,5},{5,4},{6,7},{7,6},{8,9},{9,8},{10,11... | collective-permute-start | bytes 1769480 | tf_op jit(solution)/shard_map/ppermute | solution.py:78
  62.1 16.5 %collective-permute-start.14 = (bf16[4,96,1024]{2,1,0:T(8,128)(2,1)}, bf16[4,96,1024]{2,1,0:T(8,128)(2,1)}, u32[]{:S(2)}, u32[]{:S(2)}) collective-permute-start(bf16[4,96,1024]{2,1,0:T(8,128)(2,1)} %constant_dynamic-update-slice_fusion.3.refs_0_), channel_id=1, source_target_pairs={{0,4},{1,3},{2,6},{3,1},{4,0},{5,7},{6,2},{7,5},{8,12},{9,11},{10,... | collective-permute-start | bytes 2359304 | tf_op jit(solution)/shard_map/ppermute | solution.py:78
  62.5 19.7 %collective-permute-start.20 = (bf16[4,96,1024]{2,1,0:T(8,128)(2,1)}, bf16[4,96,1024]{2,1,0:T(8,128)(2,1)}, u32[]{:S(2)}, u32[]{:S(2)}) collective-permute-start(bf16[4,96,1024]{2,1,0:T(8,128)(2,1)} %constant_dynamic-update-slice_fusion.3.refs_0_), channel_id=1, source_target_pairs={{0,1},{1,0},{2,3},{3,2},{4,5},{5,4},{6,7},{7,6},{8,9},{9,8},{10,11... | collective-permute-start | bytes 2359304 | tf_op jit(solution)/shard_map/ppermute | solution.py:78
  65.5 16.7 %collective-permute-start.23 = (bf16[4,96,512]{2,1,0:T(8,128)(2,1)}, bf16[4,96,512]{2,1,0:T(8,128)(2,1)}, u32[]{:S(2)}, u32[]{:S(2)}) collective-permute-start(bf16[4,96,512]{2,1,0:T(8,128)(2,1)} %collective-permute-done.8.refs_9_), channel_id=1, source_target_pairs={{0,1},{1,0},{2,3},{3,2},{4,5},{5,4},{6,7},{7,6},{8,9},{9,8},{10,11... | collective-permute-start | bytes 1179656 | tf_op jit(solution)/shard_map/ppermute | solution.py:78
  78.1 22.6 %collective-permute-start.17 = (bf16[4,96,1024]{2,1,0:T(8,128)(2,1)}, bf16[4,96,1024]{2,1,0:T(8,128)(2,1)}, u32[]{:S(2)}, u32[]{:S(2)}) collective-permute-start(bf16[4,96,1024]{2,1,0:T(8,128)(2,1)} %constant_dynamic-update-slice_fusion.3.refs_0_), channel_id=1, source_target_pairs={{0,2},{1,5},{2,0},{3,7},{4,6},{5,1},{6,4},{7,3},{8,10},{9,13},{10,... | collective-permute-start | bytes 2359304 | tf_op jit(solution)/shard_map/ppermute | solution.py:78
  78.6 22.2 %collective-permute-start.24 = (bf16[4,96,512]{2,1,0:T(8,128)(2,1)}, bf16[4,96,512]{2,1,0:T(8,128)(2,1)}, u32[]{:S(2)}, u32[]{:S(2)}) collective-permute-start(bf16[4,96,512]{2,1,0:T(8,128)(2,1)} %collective-permute-done.15.refs_10_), channel_id=1, source_target_pairs={{0,1},{1,0},{2,3},{3,2},{4,5},{5,4},{6,7},{7,6},{8,9},{9,8},{10,11... | collective-permute-start | bytes 1179656 | tf_op jit(solution)/shard_map/ppermute | solution.py:78
  78.6 22.2 %collective-permute-start.19 = (bf16[4,96,512]{2,1,0:T(8,128)(2,1)}, bf16[4,96,512]{2,1,0:T(8,128)(2,1)}, u32[]{:S(2)}, u32[]{:S(2)}) collective-permute-start(bf16[4,96,512]{2,1,0:T(8,128)(2,1)} %collective-permute-done.15.refs_10_), channel_id=1, source_target_pairs={{0,8},{1,9},{2,10},{3,11},{4,12},{5,13},{6,14},{7,15},{8,24},{9,25... | collective-permute-start | bytes 1179656 | tf_op jit(solution)/shard_map/ppermute | solution.py:78
  82.2 18.6 %collective-permute-start.21 = (bf16[4,96,1024]{2,1,0:T(8,128)(2,1)}, bf16[4,96,1024]{2,1,0:T(8,128)(2,1)}, u32[]{:S(2)}, u32[]{:S(2)}) collective-permute-start(bf16[4,96,1024]{2,1,0:T(8,128)(2,1)} %collective-permute-done.14.refs_1_), channel_id=1, source_target_pairs={{0,1},{1,0},{2,3},{3,2},{4,5},{5,4},{6,7},{7,6},{8,9},{9,8},{10,11... | collective-permute-start | bytes 2359304 | tf_op jit(solution)/shard_map/ppermute | solution.py:78
  82.2 18.6 %collective-permute-start.18 = (bf16[4,96,1024]{2,1,0:T(8,128)(2,1)}, bf16[4,96,1024]{2,1,0:T(8,128)(2,1)}, u32[]{:S(2)}, u32[]{:S(2)}) collective-permute-start(bf16[4,96,1024]{2,1,0:T(8,128)(2,1)} %collective-permute-done.14.refs_1_), channel_id=1, source_target_pairs={{0,2},{1,5},{2,0},{3,7},{4,6},{5,1},{6,4},{7,3},{8,10},{9,13},{10,... | collective-permute-start | bytes 2359304 | tf_op jit(solution)/shard_map/ppermute | solution.py:78
  167.5 26.7 %collective-permute-start.30 = (bf16[8,96,896]{2,1,0:T(8,128)(2,1)}, bf16[8,96,896]{2,1,0:T(8,128)(2,1)}, u32[]{:S(2)}, u32[]{:S(2)}) collective-permute-start(bf16[8,96,896]{2,1,0:T(8,128)(2,1)} %get-tuple-element.202), channel_id=1, source_target_pairs={{0,2},{1,5},{2,0},{3,7},{4,6},{5,1},{6,4},{7,3},{8,10},{9,13},{10,... | collective-permute-start | bytes 4128776 | tf_op jit(solution)/shard_map/ppermute | solution.py:78
  167.9 44.4 %collective-permute-start.32 = (bf16[8,96,768]{2,1,0:T(8,128)(2,1)}, bf16[8,96,768]{2,1,0:T(8,128)(2,1)}, u32[]{:S(2)}, u32[]{:S(2)}) collective-permute-start(bf16[8,96,768]{2,1,0:T(8,128)(2,1)} %get-tuple-element.214), channel_id=1, source_target_pairs={{0,2},{1,5},{2,0},{3,7},{4,6},{5,1},{6,4},{7,3},{8,10},{9,13},{10,... | collective-permute-start | bytes 3538952 | tf_op jit(solution)/shard_map/ppermute | solution.py:78
  196.6 15.8 %collective-permute-start.31 = (bf16[4,96,896]{2,1,0:T(8,128)(2,1)}, bf16[4,96,896]{2,1,0:T(8,128)(2,1)}, u32[]{:S(2)}, u32[]{:S(2)}) collective-permute-start(bf16[4,96,896]{2,1,0:T(8,128)(2,1)} %sums.6), channel_id=1, source_target_pairs={{0,4},{1,3},{2,6},{3,1},{4,0},{5,7},{6,2},{7,5},{8,12},{9,11},{10,... | collective-permute-start | bytes 2064392 | tf_op jit(solution)/shard_map/ppermute | solution.py:78
  219.1 20.8 %collective-permute-start.34 = (bf16[8,96,640]{2,1,0:T(8,128)(2,1)}, bf16[8,96,640]{2,1,0:T(8,128)(2,1)}, u32[]{:S(2)}, u32[]{:S(2)}) collective-permute-start(bf16[8,96,640]{2,1,0:T(8,128)(2,1)} %sums.8), channel_id=1, source_target_pairs={{0,2},{1,5},{2,0},{3,7},{4,6},{5,1},{6,4},{7,3},{8,10},{9,13},{10,... | collective-permute-start | bytes 2949128 | tf_op jit(solution)/shard_map/ppermute | solution.py:78
  220.7 16.6 %collective-permute-start.35 = (bf16[4,96,768]{2,1,0:T(8,128)(2,1)}, bf16[4,96,768]{2,1,0:T(8,128)(2,1)}, u32[]{:S(2)}, u32[]{:S(2)}) collective-permute-start(bf16[4,96,768]{2,1,0:T(8,128)(2,1)} %get-tuple-element.230), channel_id=1, source_target_pairs={{0,4},{1,3},{2,6},{3,1},{4,0},{5,7},{6,2},{7,5},{8,12},{9,11},{10,... | collective-permute-start | bytes 1769480 | tf_op jit(solution)/shard_map/ppermute | solution.py:78
  221.2 22.2 %collective-permute-start.38 = (bf16[2,96,896]{2,1,0:T(8,128)(2,1)}, bf16[2,96,896]{2,1,0:T(8,128)(2,1)}, u32[]{:S(2)}, u32[]{:S(2)}) collective-permute-start(bf16[2,96,896]{2,1,0:T(8,128)(2,1)} %get-tuple-element.245), channel_id=1, source_target_pairs={{0,16},{1,17},{2,18},{3,19},{4,20},{5,21},{6,22},{7,23},{8,24},{9,... | collective-permute-start | bytes 1032200 | tf_op jit(solution)/shard_map/ppermute | solution.py:78
  245.6 23.6 %collective-permute-start.43 = (bf16[2,96,768]{2,1,0:T(8,128)(2,1)}, bf16[2,96,768]{2,1,0:T(8,128)(2,1)S(1)}, u32[]{:S(2)}, u32[]{:S(2)}) collective-permute-start(bf16[2,96,768]{2,1,0:T(8,128)(2,1)} %get-tuple-element.253), channel_id=1, source_target_pairs={{0,16},{1,17},{2,18},{3,19},{4,20},{5,21},{6,22},{7,23},{8,24},{9,... | collective-permute-start | bytes 884744 | tf_op jit(solution)/shard_map/ppermute | solution.py:78
  251.7 19.9 %collective-permute-start.44 = (bf16[1,96,896]{2,1,0:T(8,128)(2,1)S(1)}, bf16[1,96,896]{2,1,0:T(8,128)(2,1)S(1)}, u32[]{:S(2)}, u32[]{:S(2)}) collective-permute-start(bf16[1,96,896]{2,1,0:T(8,128)(2,1)S(1)} %add_convert_fusion.1), channel_id=1, source_target_pairs={{0,8},{1,9},{2,10},{3,11},{4,12},{5,13},{6,14},{7,15},{8,0},{9,1},... | collective-permute-start | bytes 516104 | tf_op jit(solution)/shard_map/ppermute | solution.py:78
  253.6 16.7 %collective-permute-start.42 = (f32[12,768]{1,0:T(8,128)S(1)}, f32[12,768]{1,0:T(8,128)S(1)}, u32[]{:S(2)}, u32[]{:S(2)}) collective-permute-start(f32[12,768]{1,0:T(8,128)S(1)} %add.67), channel_id=1, source_target_pairs={{0,16},{1,17},{2,18},{3,19},{4,20},{5,21},{6,22},{7,23},{8,24},{9,... | collective-permute-start | bytes 110600 | tf_op jit(solution)/shard_map/ppermute | solution.py:78
  255.3 19.3 %collective-permute-start.41 = (bf16[2,96,640]{2,1,0:T(8,128)(2,1)S(1)}, bf16[2,96,640]{2,1,0:T(8,128)(2,1)S(1)}, u32[]{:S(2)}, u32[]{:S(2)}) collective-permute-start(bf16[2,96,640]{2,1,0:T(8,128)(2,1)S(1)} %add_convert_fusion), channel_id=1, source_target_pairs={{0,16},{1,17},{2,18},{3,19},{4,20},{5,21},{6,22},{7,23},{8,24},{9,... | collective-permute-start | bytes 737288 | tf_op jit(solution)/shard_map/ppermute | solution.py:78
  (50 other events, 418.7 us)

commit v3 on v2

--- a/solution.py
+++ b/solution.py
@@ -663,7 +663,7 @@
             d_norm[r, :] = jnp.zeros((TILE, width), F32)
             return 0
 
-        lax.fori_loop(0, tiles, body, 0)
+        lax.fori_loop(0, tiles, body, 0, unroll=2)
         pltpu.make_async_copy(resid_ref, resid_out, out_sems.at[0]).start()
 
     wait_all(raw.at[step], sems.at[step])

time: 287 us -> 288 us (level)
  transfers between devices with their start and end apart: 48 -> 48, of which waited for: 16 -> 16; matrix products, arithmetic and copies ran while one was open for 7% -> 7% of each run, Pallas kernels for 35% -> 34%
where the time goes in v3:
time: 288 us; the launch traced here: 287 us
  Pallas kernels  154 us (53%)
  waiting for transfers between devices  61.3 us (21%)
  starting transfers between devices  44.8 us (16%)
  local copies, waits for them, and re-layouts  13.8 us (5%)
  other arithmetic  11.2 us (4%)
    ppermute x48, waiting for transfers between devices, exchange(): return lax.ppermute(array, BOTH, pairs)  61.3 us
    pallas_call x1, Pallas kernels, feed_forward(): pl.pallas_call(functools.partial(feed_kernel, counts), grid_spec=pltpu.Pr...  46.1 us
    ppermute x48, starting transfers between devices, exchange(): return lax.ppermute(array, BOTH, pairs)  44.8 us
    pallas_call x2, Pallas kernels, attend_back(): pl.pallas_call(functools.partial(attend_back_kernel, first, len(grads), b...  39.9 us
    pallas_call x1, Pallas kernels, attend(): pl.pallas_call(attend_kernel, grid_spec=pltpu.PrefetchScalarGridSpec(num_...  16.8 us
    pallas_call x5, Pallas kernels, sums(): pl.pallas_call(functools.partial(sums_kernel, plan), in_specs=[ANY_SPEC]...  14.4 us
    pallas_call x1, Pallas kernels, project(): pl.pallas_call(functools.partial(qkv_kernel, len(sources)), grid_spec=plt...  12.1 us
    pallas_call x1, Pallas kernels, hidden_rows(): pl.pallas_call(functools.partial(hidden_kernel, counts), grid_spec=pltpu....  11.8 us
  transfers between devices with their start and end apart: 48, of which 16 were waited for; matrix products, arithmetic and copies ran while one was open for 7% of the time, Pallas kernels for 34%

profile of v3, /device:TPU:0, one launch (start us, length us, event | category | flops | bytes accessed | tf_op | source)
XLA Modules:
  0.0 286.8 jit_solution(8789909371036330565)
XLA Ops:
  3.1 3.1 %collective-permute-start = (bf16[1,96,768]{2,1,0:T(8,128)(2,1)S(1)}, bf16[1,96,768]{2,1,0:T(8,128)(2,1)S(1)}, u32[]{:S(2)}, u32[]{:S(2)}) collective-permute-start(bf16[1,96,768]{2,1,0:T(8,128)(2,1)S(1)} %bitcast.37), channel_id=1, source_target_pairs={{0,8},{1,9},{2,10},{3,11},{4,12},{5,13},{6,14},{7,15},{8,0},{9,1},... | collective-permute-start | bytes 442376 | tf_op jit(solution)/shard_map/ppermute | solution.py:78
  23.1 5.1 %collective-permute-done.4 = bf16[1,96,1024]{2,1,0:T(8,128)(2,1)S(1)} collective-permute-done((bf16[1,96,1024]{2,1,0:T(8,128)(2,1)S(1)}, bf16[1,96,1024]{2,1,0:T(8,128)(2,1)S(1)}, u32[]{:S(2)}, u32[]{:S(2)}) %collective-permute-start.4) | collective-permute-done | bytes 196640 | tf_op jit(solution)/shard_map/ppermute | solution.py:78
  28.2 4.0 %collective-permute-done.1 = bf16[2,96,768]{2,1,0:T(8,128)(2,1)S(1)} collective-permute-done((bf16[2,96,768]{2,1,0:T(8,128)(2,1)S(1)}, bf16[2,96,768]{2,1,0:T(8,128)(2,1)S(1)}, u32[]{:S(2)}, u32[]{:S(2)}) %collective-permute-start.1) | collective-permute-done | bytes 294944 | tf_op jit(solution)/shard_map/ppermute | solution.py:78
  36.5 3.4 %collective-permute-start.7 = (bf16[1,96,1024]{2,1,0:T(8,128)(2,1)S(1)}, bf16[1,96,1024]{2,1,0:T(8,128)(2,1)S(1)}, u32[]{:S(2)}, u32[]{:S(2)}) collective-permute-start(bf16[1,96,1024]{2,1,0:T(8,128)(2,1)S(1)} %collective-permute-done.4), channel_id=1, source_target_pairs={{0,8},{1,9},{2,10},{3,11},{4,12},{5,13},{6,14},{7,15},{8,24},{9,25... | collective-permute-start | bytes 589832 | tf_op jit(solution)/shard_map/ppermute | solution.py:78
  39.9 10.3 %collective-permute-done.7 = bf16[1,96,1024]{2,1,0:T(8,128)(2,1)S(1)} collective-permute-done((bf16[1,96,1024]{2,1,0:T(8,128)(2,1)S(1)}, bf16[1,96,1024]{2,1,0:T(8,128)(2,1)S(1)}, u32[]{:S(2)}, u32[]{:S(2)}) %collective-permute-start.7) | collective-permute-done | bytes 196640 | tf_op jit(solution)/shard_map/ppermute | solution.py:78
  54.6 4.6 %collective-permute-done.10 = bf16[1,96,1024]{2,1,0:T(8,128)(2,1)S(1)} collective-permute-done((bf16[1,96,1024]{2,1,0:T(8,128)(2,1)S(1)}, bf16[1,96,1024]{2,1,0:T(8,128)(2,1)S(1)}, u32[]{:S(2)}, u32[]{:S(2)}) %collective-permute-start.10) | collective-permute-done | bytes 196640 | tf_op jit(solution)/shard_map/ppermute | solution.py:78
  66.0 12.1 %project.1 = (bf16[1024,768]{1,0:T(8,128)(2,1)}, bf16[1024,768]{1,0:T(8,128)(2,1)}, bf16[1024,768]{1,0:T(8,128)(2,1)}, bf16[1024,768]{1,0:T(8,128)(2,1)}, bf16[4,768,768]{2,1,0:T(8,128)(2,1)}) custom-call(s32[4]{0:T(128)} %pad_add_fusion.place_ref, bf16[1024,768]{1,0:T(8,128)(2,1)} %refs_7_.1, f32[1,768]{1,0:T(1,128)} %broadcast_in_dim.13.gain_ref.refs_9_, ...), custom_call_target="tpu_custom_call" | custom-call | flops 3623878656 | bytes 12582912 | tf_op jit(solution)/shard_map/project/pallas_call | solution.py:362
  78.6 3.6 %collective-permute-start.19 = (bf16[4,96,512]{2,1,0:T(8,128)(2,1)}, bf16[4,96,512]{2,1,0:T(8,128)(2,1)}, u32[]{:S(2)}, u32[]{:S(2)}) collective-permute-start(bf16[4,96,512]{2,1,0:T(8,128)(2,1)} %collective-permute-done.15.refs_10_), channel_id=1, source_target_pairs={{0,8},{1,9},{2,10},{3,11},{4,12},{5,13},{6,14},{7,15},{8,24},{9,25... | collective-permute-start | bytes 1179656 | tf_op jit(solution)/shard_map/ppermute | solution.py:78
  84.0 16.8 %attend.1 = (bf16[1024,768]{1,0:T(8,128)(2,1)}, f32[6,8,1024]{2,1,0:T(8,128)}) custom-call(s32[1]{0:T(128)} %dynamic_slice.6.len_ref, bf16[1024,768]{1,0:T(8,128)(2,1)} %get-tuple-element.174.q_ref, bf16[1024,768]{1,0:T(8,128)(2,1)} %get-tuple-element.175.k_ref, bf16[1024,768]{1,0:T(8,128)(2,1)} %get-tuple-element.176.v_ref), custom_call_target="tpu_custom_call" | custom-call | flops 16000000000 | bytes 6291456 | tf_op jit(solution)/shard_map/attend/pallas_call | solution.py:445
  101.5 3.7 %collective-permute-done.27.refs_15_ = bf16[4,96,512]{2,1,0:T(8,128)(2,1)} collective-permute-done((bf16[4,96,512]{2,1,0:T(8,128)(2,1)}, bf16[4,96,512]{2,1,0:T(8,128)(2,1)}, u32[]{:S(2)}, u32[]{:S(2)}) %collective-permute-start.27) | collective-permute-done | bytes 393248 | tf_op jit(solution)/shard_map/ppermute | solution.py:78
  105.2 46.1 %feed_forward.1 = (f32[1024,768]{1,0:T(8,128)}, bf16[1024,3072]{1,0:T(8,128)(2,1)}, f32[4,1,768]{2,1,0:T(1,128)}, f32[1024,768]{1,0:T(8,128)}, bf16[1024,768]{1,...) custom-call(s32[4]{0:T(128)} %pad_add_fusion.place_ref, ...), custom_call_target="tpu_custom_call" | custom-call | flops 40000000000 | bytes 40000000 | tf_op jit(solution)/shard_map/feed_forward/pallas_call | solution.py:750
  152.5 11.8 %hidden_rows.1 = bf16[1024,768]{1,0:T(8,128)(2,1)} custom-call(s32[4]{0:T(128)} %pad_add_fusion.place_ref, bf16[1024,3072]{1,0:T(8,128)(2,1)} %get-tuple-element.195.act_ref, f32[1024,768]{1,0:T(8,128)} %get-tuple-element.196.resid_ref, f32[8,768]{1,0:T(8,128)} %stack.43.vec_ref, bf16[4,96,1024]{2,1,0:T(8,128)(2,1)} %constant_dynamic-update-slice_fusion.3.refs_0_, ...), custom_call_target="tpu_custom_call" | custom-call | flops 5000000000 | bytes 12000000 | tf_op jit(solution)/shard_map/hidden_rows/pallas_call | solution.py:835
  164.3 4.0 %sums.5 = (bf16[8,96,896]{2,1,0:T(8,128)(2,1)}, bf16[8,96,768]{2,1,0:T(8,128)(2,1)}) custom-call(bf16[16,96,896]{2,1,0:T(8,128)(2,1)} %get-tuple-element.198.refs_0_, bf16[16,96,896]{2,1,0:T(8,128)(2,1)} %collective-permute-done.28.refs_1_, bf16[16,96,768]{2,1,0:T(8,128)(2,1)} %get-tuple-element.200.refs_2_.refs_4_.refs_3_.refs_6_, ...), custom_call_target="tpu_custom_call" | custom-call | flops 1000000 | bytes 8000000 | tf_op jit(solution)/shard_map/sums/pallas_call | solution.py:145
  170.4 24.6 %attend_back.2 = (bf16[1024,512]{1,0:T(8,128)(2,1)}, bf16[1024,512]{1,0:T(8,128)(2,1)}, bf16[1024,512]{1,0:T(8,128)(2,1)}, bf16[16,96,640]{2,1,0:T(8,128)(2,1)}, bf16[16,96,640]{2,1,0:T(8,128)(2,1)}) custom-call(s32[1]{0:T(128)} %dynamic_slice.6.len_ref, s32[4]{0:T(128)} %pad_add_fusion.place_ref, bf16[1024,768]{1,0:T(8,128)(2,1)} %get-tuple-element.174.q_ref, ...), custom_call_target="tpu_custom_call" | custom-call | flops 12000000000 | bytes 20000000 | tf_op jit(solution)/shard_map/attend_back/pallas_call | solution.py:577
  197.8 15.3 %attend_back.3 = (bf16[1024,256]{1,0:T(8,128)(2,1)}, bf16[1024,256]{1,0:T(8,128)(2,1)}, bf16[1024,256]{1,0:T(8,128)(2,1)}, bf16[16,96,640]{2,1,0:T(8,128)(2,1)}, bf16[16,96,640]{2,1,0:T(8,128)(2,1)}) custom-call(s32[1]{0:T(128)} %dynamic_slice.6.len_ref, s32[4]{0:T(128)} %pad_add_fusion.place_ref, ...), custom_call_target="tpu_custom_call", output_to_operand_aliasing={{3}: (10, {}), {4}: (11, {})} | custom-call | flops 6000000000 | bytes 10000000 | tf_op jit(solution)/shard_map/attend_back/pallas_call | solution.py:577
  213.3 2.9 %sums.7 = (bf16[2,96,896]{2,1,0:T(8,128)(2,1)}, bf16[4,96,768]{2,1,0:T(8,128)(2,1)}) custom-call(bf16[16,96,896]{2,1,0:T(8,128)(2,1)} %get-tuple-element.198.refs_0_, bf16[16,96,896]{2,1,0:T(8,128)(2,1)} %collective-permute-done.28.refs_1_, bf16[8,96,896]{2,1,0:T(8,128)(2,1)} %collective-permute-done.30.refs_2_, ...), custom_call_target="tpu_custom_call" | custom-call | flops 1000000 | bytes 8000000 | tf_op jit(solution)/shard_map/sums/pallas_call | solution.py:145
  222.5 10.1 %input_grad.1 = (f32[1024,768]{1,0:T(8,128)}, f32[8,768]{1,0:T(8,128)}) custom-call(bf16[1024,512]{1,0:T(8,128)(2,1)} %get-tuple-element.231.refs_0_, bf16[1024,512]{1,0:T(8,128)(2,1)} %get-tuple-element.232.refs_1_, bf16[1024,512]{1,0:T(8,128)(2,1)} %get-tuple-element.233.refs_2_, bf16[1024,256]{1,0:T(8,128)(2,1)} %get-tuple-element.234.refs_3_, ...), custom_call_target="tpu_custom_call" | custom-call | flops 3623878656 | bytes 12582912 | tf_op jit(solution)/shard_map/input_grad/pallas_call | solution.py:884
  232.6 5.7 %collective-permute-done.35.refs_6_.refs_9_ = bf16[4,96,768]{2,1,0:T(8,128)(2,1)} collective-permute-done((bf16[4,96,768]{2,1,0:T(8,128)(2,1)}, bf16[4,96,768]{2,1,0:T(8,128)(2,1)}, u32[]{:S(2)}, u32[]{:S(2)}) %collective-permute-start.35) | collective-permute-done | bytes 589856 | tf_op jit(solution)/shard_map/ppermute | solution.py:78
  241.5 2.7 sums.9
  246.8 3.1 %collective-permute-done.37 = f32[12,768]{1,0:T(8,128)S(1)} collective-permute-done((f32[12,768]{1,0:T(8,128)S(1)}, f32[12,768]{1,0:T(8,128)S(1)}, u32[]{:S(2)}, u32[]{:S(2)}) %collective-permute-start.37) | collective-permute-done | bytes 36896 | tf_op jit(solution)/shard_map/ppermute | solution.py:78
  256.1 2.6 collective-permute-start.41
  258.8 11.3 %collective-permute-done.43.refs_10_ = bf16[2,96,768]{2,1,0:T(8,128)(2,1)S(1)} collective-permute-done((bf16[2,96,768]{2,1,0:T(8,128)(2,1)}, bf16[2,96,768]{2,1,0:T(8,128)(2,1)S(1)}, u32[]{:S(2)}, u32[]{:S(2)}) %collective-permute-start.43) | collective-permute-done | bytes 294944 | tf_op jit(solution)/shard_map/ppermute | solution.py:78
  272.4 3.1 %collective-permute-done.41.refs_16_ = bf16[2,96,640]{2,1,0:T(8,128)(2,1)S(1)} collective-permute-done((bf16[2,96,640]{2,1,0:T(8,128)(2,1)S(1)}, bf16[2,96,640]{2,1,0:T(8,128)(2,1)S(1)}, u32[]{:S(2)}, u32[]{:S(2)}) %collective-permute-start.41) | collective-permute-done | bytes 245792 | tf_op jit(solution)/shard_map/ppermute | solution.py:78
  283.7 2.8 last_sums.1
  (200 shorter events, 72.3 us)
Async XLA Ops:
  13.2 15.1 %collective-permute-start.4 = (bf16[1,96,1024]{2,1,0:T(8,128)(2,1)S(1)}, bf16[1,96,1024]{2,1,0:T(8,128)(2,1)S(1)}, u32[]{:S(2)}, u32[]{:S(2)}) collective-permute-start(bf16[1,96,1024]{2,1,0:T(8,128)(2,1)S(1)} %pad_maximum_fusion.2), channel_id=1, source_target_pairs={{0,8},{1,9},{2,10},{3,11},{4,12},{5,13},{6,14},{7,15},{8,24},{9,25... | collective-permute-start | bytes 589832 | tf_op jit(solution)/shard_map/ppermute | solution.py:78
  14.8 17.4 %collective-permute-start.1 = (bf16[2,96,768]{2,1,0:T(8,128)(2,1)S(1)}, bf16[2,96,768]{2,1,0:T(8,128)(2,1)S(1)}, u32[]{:S(2)}, u32[]{:S(2)}) collective-permute-start(bf16[2,96,768]{2,1,0:T(8,128)(2,1)S(1)} %pad_maximum_fusion.1), channel_id=1, source_target_pairs={{0,16},{1,17},{2,18},{3,19},{4,20},{5,21},{6,22},{7,23},{8,24},{9,... | collective-permute-start | bytes 884744 | tf_op jit(solution)/shard_map/ppermute | solution.py:78
  32.3 17.9 %collective-permute-start.6 = (bf16[4,96,768]{2,1,0:T(8,128)(2,1)S(1)}, bf16[4,96,768]{2,1,0:T(8,128)(2,1)S(1)}, u32[]{:S(2)}, u32[]{:S(2)}) collective-permute-start(bf16[4,96,768]{2,1,0:T(8,128)(2,1)S(1)} %pad_maximum_fusion.refs_0_), channel_id=1, source_target_pairs={{0,2},{1,5},{2,0},{3,7},{4,6},{5,1},{6,4},{7,3},{8,10},{9,13},{10,... | collective-permute-start | bytes 1769480 | tf_op jit(solution)/shard_map/ppermute | solution.py:78
  33.0 17.2 %collective-permute-start.5 = (bf16[4,96,768]{2,1,0:T(8,128)(2,1)S(1)}, bf16[4,96,768]{2,1,0:T(8,128)(2,1)S(1)}, u32[]{:S(2)}, u32[]{:S(2)}) collective-permute-start(bf16[4,96,768]{2,1,0:T(8,128)(2,1)S(1)} %pad_maximum_fusion.refs_0_), channel_id=1, source_target_pairs={{0,4},{1,3},{2,6},{3,1},{4,0},{5,7},{6,2},{7,5},{8,12},{9,11},{10,... | collective-permute-start | bytes 1769480 | tf_op jit(solution)/shard_map/ppermute | solution.py:78
  35.7 14.5 %collective-permute-start.8 = (bf16[4,96,512]{2,1,0:T(8,128)(2,1)}, bf16[4,96,512]{2,1,0:T(8,128)(2,1)}, u32[]{:S(2)}, u32[]{:S(2)}) collective-permute-start(bf16[4,96,512]{2,1,0:T(8,128)(2,1)} %constant_dynamic-update-slice_fusion.refs_8_), channel_id=1, source_target_pairs={{0,8},{1,9},{2,10},{3,11},{4,12},{5,13},{6,14},{7,15},{8,24},{9,25... | collective-permute-start | bytes 1179656 | tf_op jit(solution)/shard_map/ppermute | solution.py:78
  39.9 14.7 %collective-permute-start.11 = (bf16[4,96,768]{2,1,0:T(8,128)(2,1)S(1)}, bf16[4,96,768]{2,1,0:T(8,128)(2,1)S(1)}, u32[]{:S(2)}, u32[]{:S(2)}) collective-permute-start(bf16[4,96,768]{2,1,0:T(8,128)(2,1)S(1)} %pad_maximum_fusion.refs_0_), channel_id=1, source_target_pairs={{0,1},{1,0},{2,3},{3,2},{4,5},{5,4},{6,7},{7,6},{8,9},{9,8},{10,11... | collective-permute-start | bytes 1769480 | tf_op jit(solution)/shard_map/ppermute | solution.py:78
  62.1 16.5 %collective-permute-start.14 = (bf16[4,96,1024]{2,1,0:T(8,128)(2,1)}, bf16[4,96,1024]{2,1,0:T(8,128)(2,1)}, u32[]{:S(2)}, u32[]{:S(2)}) collective-permute-start(bf16[4,96,1024]{2,1,0:T(8,128)(2,1)} %constant_dynamic-update-slice_fusion.3.refs_0_), channel_id=1, source_target_pairs={{0,4},{1,3},{2,6},{3,1},{4,0},{5,7},{6,2},{7,5},{8,12},{9,11},{10,... | collective-permute-start | bytes 2359304 | tf_op jit(solution)/shard_map/ppermute | solution.py:78
  62.5 19.7 %collective-permute-start.20 = (bf16[4,96,1024]{2,1,0:T(8,128)(2,1)}, bf16[4,96,1024]{2,1,0:T(8,128)(2,1)}, u32[]{:S(2)}, u32[]{:S(2)}) collective-permute-start(bf16[4,96,1024]{2,1,0:T(8,128)(2,1)} %constant_dynamic-update-slice_fusion.3.refs_0_), channel_id=1, source_target_pairs={{0,1},{1,0},{2,3},{3,2},{4,5},{5,4},{6,7},{7,6},{8,9},{9,8},{10,11... | collective-permute-start | bytes 2359304 | tf_op jit(solution)/shard_map/ppermute | solution.py:78
  65.5 16.7 %collective-permute-start.23 = (bf16[4,96,512]{2,1,0:T(8,128)(2,1)}, bf16[4,96,512]{2,1,0:T(8,128)(2,1)}, u32[]{:S(2)}, u32[]{:S(2)}) collective-permute-start(bf16[4,96,512]{2,1,0:T(8,128)(2,1)} %collective-permute-done.8.refs_9_), channel_id=1, source_target_pairs={{0,1},{1,0},{2,3},{3,2},{4,5},{5,4},{6,7},{7,6},{8,9},{9,8},{10,11... | collective-permute-start | bytes 1179656 | tf_op jit(solution)/shard_map/ppermute | solution.py:78
  78.1 22.6 %collective-permute-start.17 = (bf16[4,96,1024]{2,1,0:T(8,128)(2,1)}, bf16[4,96,1024]{2,1,0:T(8,128)(2,1)}, u32[]{:S(2)}, u32[]{:S(2)}) collective-permute-start(bf16[4,96,1024]{2,1,0:T(8,128)(2,1)} %constant_dynamic-update-slice_fusion.3.refs_0_), channel_id=1, source_target_pairs={{0,2},{1,5},{2,0},{3,7},{4,6},{5,1},{6,4},{7,3},{8,10},{9,13},{10,... | collective-permute-start | bytes 2359304 | tf_op jit(solution)/shard_map/ppermute | solution.py:78
  78.6 22.2 %collective-permute-start.24 = (bf16[4,96,512]{2,1,0:T(8,128)(2,1)}, bf16[4,96,512]{2,1,0:T(8,128)(2,1)}, u32[]{:S(2)}, u32[]{:S(2)}) collective-permute-start(bf16[4,96,512]{2,1,0:T(8,128)(2,1)} %collective-permute-done.15.refs_10_), channel_id=1, source_target_pairs={{0,1},{1,0},{2,3},{3,2},{4,5},{5,4},{6,7},{7,6},{8,9},{9,8},{10,11... | collective-permute-start | bytes 1179656 | tf_op jit(solution)/shard_map/ppermute | solution.py:78
  78.6 22.2 %collective-permute-start.19 = (bf16[4,96,512]{2,1,0:T(8,128)(2,1)}, bf16[4,96,512]{2,1,0:T(8,128)(2,1)}, u32[]{:S(2)}, u32[]{:S(2)}) collective-permute-start(bf16[4,96,512]{2,1,0:T(8,128)(2,1)} %collective-permute-done.15.refs_10_), channel_id=1, source_target_pairs={{0,8},{1,9},{2,10},{3,11},{4,12},{5,13},{6,14},{7,15},{8,24},{9,25... | collective-permute-start | bytes 1179656 | tf_op jit(solution)/shard_map/ppermute | solution.py:78
  82.2 18.6 %collective-permute-start.21 = (bf16[4,96,1024]{2,1,0:T(8,128)(2,1)}, bf16[4,96,1024]{2,1,0:T(8,128)(2,1)}, u32[]{:S(2)}, u32[]{:S(2)}) collective-permute-start(bf16[4,96,1024]{2,1,0:T(8,128)(2,1)} %collective-permute-done.14.refs_1_), channel_id=1, source_target_pairs={{0,1},{1,0},{2,3},{3,2},{4,5},{5,4},{6,7},{7,6},{8,9},{9,8},{10,11... | collective-permute-start | bytes 2359304 | tf_op jit(solution)/shard_map/ppermute | solution.py:78
  82.2 18.6 %collective-permute-start.18 = (bf16[4,96,1024]{2,1,0:T(8,128)(2,1)}, bf16[4,96,1024]{2,1,0:T(8,128)(2,1)}, u32[]{:S(2)}, u32[]{:S(2)}) collective-permute-start(bf16[4,96,1024]{2,1,0:T(8,128)(2,1)} %collective-permute-done.14.refs_1_), channel_id=1, source_target_pairs={{0,2},{1,5},{2,0},{3,7},{4,6},{5,1},{6,4},{7,3},{8,10},{9,13},{10,... | collective-permute-start | bytes 2359304 | tf_op jit(solution)/shard_map/ppermute | solution.py:78
  168.3 26.7 %collective-permute-start.30 = (bf16[8,96,896]{2,1,0:T(8,128)(2,1)}, bf16[8,96,896]{2,1,0:T(8,128)(2,1)}, u32[]{:S(2)}, u32[]{:S(2)}) collective-permute-start(bf16[8,96,896]{2,1,0:T(8,128)(2,1)} %get-tuple-element.202), channel_id=1, source_target_pairs={{0,2},{1,5},{2,0},{3,7},{4,6},{5,1},{6,4},{7,3},{8,10},{9,13},{10,... | collective-permute-start | bytes 4128776 | tf_op jit(solution)/shard_map/ppermute | solution.py:78
  168.8 44.4 %collective-permute-start.32 = (bf16[8,96,768]{2,1,0:T(8,128)(2,1)}, bf16[8,96,768]{2,1,0:T(8,128)(2,1)}, u32[]{:S(2)}, u32[]{:S(2)}) collective-permute-start(bf16[8,96,768]{2,1,0:T(8,128)(2,1)} %get-tuple-element.214), channel_id=1, source_target_pairs={{0,2},{1,5},{2,0},{3,7},{4,6},{5,1},{6,4},{7,3},{8,10},{9,13},{10,... | collective-permute-start | bytes 3538952 | tf_op jit(solution)/shard_map/ppermute | solution.py:78
  197.4 15.8 %collective-permute-start.31 = (bf16[4,96,896]{2,1,0:T(8,128)(2,1)}, bf16[4,96,896]{2,1,0:T(8,128)(2,1)}, u32[]{:S(2)}, u32[]{:S(2)}) collective-permute-start(bf16[4,96,896]{2,1,0:T(8,128)(2,1)} %sums.6), channel_id=1, source_target_pairs={{0,4},{1,3},{2,6},{3,1},{4,0},{5,7},{6,2},{7,5},{8,12},{9,11},{10,... | collective-permute-start | bytes 2064392 | tf_op jit(solution)/shard_map/ppermute | solution.py:78
  219.9 20.8 %collective-permute-start.34 = (bf16[8,96,640]{2,1,0:T(8,128)(2,1)}, bf16[8,96,640]{2,1,0:T(8,128)(2,1)}, u32[]{:S(2)}, u32[]{:S(2)}) collective-permute-start(bf16[8,96,640]{2,1,0:T(8,128)(2,1)} %sums.8), channel_id=1, source_target_pairs={{0,2},{1,5},{2,0},{3,7},{4,6},{5,1},{6,4},{7,3},{8,10},{9,13},{10,... | collective-permute-start | bytes 2949128 | tf_op jit(solution)/shard_map/ppermute | solution.py:78
  221.7 16.6 %collective-permute-start.35 = (bf16[4,96,768]{2,1,0:T(8,128)(2,1)}, bf16[4,96,768]{2,1,0:T(8,128)(2,1)}, u32[]{:S(2)}, u32[]{:S(2)}) collective-permute-start(bf16[4,96,768]{2,1,0:T(8,128)(2,1)} %get-tuple-element.230), channel_id=1, source_target_pairs={{0,4},{1,3},{2,6},{3,1},{4,0},{5,7},{6,2},{7,5},{8,12},{9,11},{10,... | collective-permute-start | bytes 1769480 | tf_op jit(solution)/shard_map/ppermute | solution.py:78
  222.1 22.1 %collective-permute-start.38 = (bf16[2,96,896]{2,1,0:T(8,128)(2,1)}, bf16[2,96,896]{2,1,0:T(8,128)(2,1)}, u32[]{:S(2)}, u32[]{:S(2)}) collective-permute-start(bf16[2,96,896]{2,1,0:T(8,128)(2,1)} %get-tuple-element.245), channel_id=1, source_target_pairs={{0,16},{1,17},{2,18},{3,19},{4,20},{5,21},{6,22},{7,23},{8,24},{9,... | collective-permute-start | bytes 1032200 | tf_op jit(solution)/shard_map/ppermute | solution.py:78
  246.5 23.6 %collective-permute-start.43 = (bf16[2,96,768]{2,1,0:T(8,128)(2,1)}, bf16[2,96,768]{2,1,0:T(8,128)(2,1)S(1)}, u32[]{:S(2)}, u32[]{:S(2)}) collective-permute-start(bf16[2,96,768]{2,1,0:T(8,128)(2,1)} %get-tuple-element.253), channel_id=1, source_target_pairs={{0,16},{1,17},{2,18},{3,19},{4,20},{5,21},{6,22},{7,23},{8,24},{9,... | collective-permute-start | bytes 884744 | tf_op jit(solution)/shard_map/ppermute | solution.py:78
  252.5 19.9 %collective-permute-start.44 = (bf16[1,96,896]{2,1,0:T(8,128)(2,1)S(1)}, bf16[1,96,896]{2,1,0:T(8,128)(2,1)S(1)}, u32[]{:S(2)}, u32[]{:S(2)}) collective-permute-start(bf16[1,96,896]{2,1,0:T(8,128)(2,1)S(1)} %add_convert_fusion.1), channel_id=1, source_target_pairs={{0,8},{1,9},{2,10},{3,11},{4,12},{5,13},{6,14},{7,15},{8,0},{9,1},... | collective-permute-start | bytes 516104 | tf_op jit(solution)/shard_map/ppermute | solution.py:78
  254.4 16.7 %collective-permute-start.42 = (f32[12,768]{1,0:T(8,128)S(1)}, f32[12,768]{1,0:T(8,128)S(1)}, u32[]{:S(2)}, u32[]{:S(2)}) collective-permute-start(f32[12,768]{1,0:T(8,128)S(1)} %add.67), channel_id=1, source_target_pairs={{0,16},{1,17},{2,18},{3,19},{4,20},{5,21},{6,22},{7,23},{8,24},{9,... | collective-permute-start | bytes 110600 | tf_op jit(solution)/shard_map/ppermute | solution.py:78
  256.1 19.4 %collective-permute-start.41 = (bf16[2,96,640]{2,1,0:T(8,128)(2,1)S(1)}, bf16[2,96,640]{2,1,0:T(8,128)(2,1)S(1)}, u32[]{:S(2)}, u32[]{:S(2)}) collective-permute-start(bf16[2,96,640]{2,1,0:T(8,128)(2,1)S(1)} %add_convert_fusion), channel_id=1, source_target_pairs={{0,16},{1,17},{2,18},{3,19},{4,20},{5,21},{6,22},{7,23},{8,24},{9,... | collective-permute-start | bytes 737288 | tf_op jit(solution)/shard_map/ppermute | solution.py:78
  (50 other events, 419.2 us)
